TPU v7x, 256 devices: a whole 4x4x8 slice. The times are simulated.
256 devices in a mesh: plane: 8 (over z), pencil: 32 (over x, y, core).
Axes of the slice: x: 4, y: 4, z: 8, core: 2. Of those that a mesh axis runs over, the one named last changes fastest.
Arguments:
- velocity: float32 [16, 5120, 3840], P('plane', 'pencil'), may hold values from -6 to 6
- plane_slot: int32 [16], replicated, may hold values from 0 to 15, as said below
- pair_list: int32 [80, 2], replicated, may hold values from 0 to 15, as said below
Outputs:
- band_cross: float32 [16, 8, 2, 1024, 512], P('plane', None, None, 'pencil')
- partner_cross: float32 [16, 8, 2, 1024, 512], P('plane', None, None, 'pencil')
Inputs may be any that keep to these rules, and one draw needn't show every extreme that they name: Plane q is held in slot plane_slot[q] of velocity; that slot lies in the same aligned block of 2 slots as q, and every slot holds exactly one plane. `pair_list`: each row (a, b) satisfies a <= b < a + 8; no row appears twice; rows (0, 0) and (15, 15) are present.
All inputs are finite; a program needn't handle non-finite values.
Results may differ from a plain program's by a relative error of at most 0.000088.
Values sent between devices are 32-bit elements; how exact they have to be, the bound alone decides.
A program may use at most 128 MiB of HBM per device.

v0:
```python
import functools
import math

import jax
import jax.numpy as jnp
import numpy as np
from jax import lax
from jax.experimental import pallas as pl
from jax.experimental.pallas import tpu as pltpu
from jax.sharding import PartitionSpec as P

NX = 5120
NZ = 3840
KX = 512
KZ = 1024
BAND = 8
CLASSES = 16
SPAN = NZ // CLASSES
PEERS = 32
RINGS = 8
ROWS = NX // PEERS
HALF = ROWS // 2
MESH = pl.DeviceIdType.MESH
bf16 = jnp.bfloat16
f32 = jnp.float32


def split_np(table):
    high = np.asarray(table, np.float32).astype(bf16)
    low = (table - high.astype(np.float64)).astype(np.float32).astype(bf16)
    return high, low


@functools.cache
def tables():
    lane = np.arange(128)
    t0, ri, m_lo, tb = lane // 64, lane // 32 % 2, lane // 16 % 2, lane % 16
    m = 4 * tb + 2 * t0 + m_lo
    z = np.arange(256)
    phase = 2 * np.pi * ((z[:, None] * m[None, :]) % SPAN) / SPAN
    real_rows = np.where(ri == 0, np.cos(phase), -np.sin(phase))
    imag_rows = np.where(ri == 0, np.sin(phase), np.cos(phase))
    inside = (z < SPAN)[:, None]
    span = np.concatenate([real_rows * inside, imag_rows * inside], axis=0)
    span_hi, span_lo = split_np(span)

    c = np.arange(CLASSES)
    turn = 2 * np.pi * (c[:, None] * z[None, :]) / NZ
    keep = (z < SPAN)[None, :]
    twist = np.stack([np.cos(turn) * keep, np.sin(turn) * keep], axis=1).astype(np.float32)

    k = np.arange(KX)
    kx = np.where(k < KX // 2, k, k - KX)
    r = np.arange(HALF)
    theta = 2 * np.pi * ((kx[:, None] * r[None, :]) % NX) / NX
    axial = np.concatenate([np.cos(theta), np.sin(theta)], axis=0)
    ax_hi, ax_lo = split_np(axial)
    pad = np.zeros((2 * KX, 256 - 3 * HALF), bf16)
    axial_cat = np.concatenate([ax_hi, ax_hi, ax_lo, pad], axis=1)

    step = 2 * np.pi * 2 * np.arange(16) / PEERS
    back = np.stack([np.cos(step), np.sin(step)])[:, :, None] * np.ones((1, 1, 256))
    return np.stack([span_hi, span_lo]), twist, axial_cat, back.astype(np.float32)


def times(a, w):
    ar, ai = a
    wr, wi = w
    s = math.sqrt(0.5)
    if abs(wr - 1) < 1e-12:
        return a
    if abs(wr) < 1e-12 and abs(wi + 1) < 1e-12:
        return (ai, None if ar is None else -ar)
    if abs(wr - s) < 1e-12 and abs(wi + s) < 1e-12 and ai is not None:
        return ((ar + ai) * s, (ai - ar) * s)
    if ai is None:
        return (ar * wr, ar * wi)
    return (ar * wr - ai * wi, ar * wi + ai * wr)


def add(a, b):
    if a is None:
        return b
    if b is None:
        return a
    return a + b


def sub(a, b):
    if b is None:
        return a
    if a is None:
        return -b
    return a - b


def real_fft(xs):
    n = len(xs)
    if n == 1:
        return [(xs[0], None)]
    even = real_fft(xs[0::2])
    odd = real_fft(xs[1::2])
    out = [None] * (n // 2 + 1)
    for k in range(n // 4 + 1):
        w = (math.cos(2 * math.pi * k / n), -math.sin(2 * math.pi * k / n))
        er, ei = even[k]
        tr, ti = times(odd[k], w)
        out[k] = (add(er, tr), add(ei, ti))
        if n // 2 - k != k:
            out[n // 2 - k] = (sub(er, tr), sub(ti, ei))
    return out


def twisted_classes(xs, cos_of, sin_of):
    modes = real_fft(xs)
    out = []
    for c in range(CLASSES):
        a, b = modes[c] if c <= 8 else modes[16 - c]
        if c == 0:
            out.append((a, jnp.zeros_like(a)))
            continue
        tc, ts = cos_of(c), sin_of(c)
        if b is None:
            out.append((a * tc, -(a * ts)))
        elif c < 8:
            out.append((a * tc + b * ts, b * tc - a * ts))
        else:
            out.append((a * tc - b * ts, -(b * tc + a * ts)))
    return out


def split(x):
    high = x.astype(bf16)
    return high, (x - high.astype(f32)).astype(bf16)


def lane_exchange(tiles, lane, roll):
    tiles = list(tiles)
    for bit in range(4):
        gap = 1 << bit
        low_lane = (lane & gap) == 0
        for i in range(16):
            if i & gap:
                continue
            lo, hi = tiles[i], tiles[i | gap]
            tiles[i] = jnp.where(low_lane, lo, roll(hi, gap))
            tiles[i | gap] = jnp.where(low_lane, roll(lo, 128 - gap), hi)
    return tiles


def lane_roll(x, shift):
    return pltpu.roll(x, shift, 1)


def transform_kernel(
    slot_ref, vel_hbm, span_ref, twist_ref, axial_ref, back_ref, out_ref,
    vel, y_hi, y_lo, z_buf, send_buf, recv_buf, v_cat, q_buf, acc_a, acc_b,
    load_sem, own_sem, a_send, a_recv, z_send, z_recv,
):
    me = lax.axis_index("pencil")
    ring = lax.axis_index("plane")
    below = lax.rem(ring + RINGS - 1, RINGS)
    above = lax.rem(ring + 1, RINGS)

    barrier = pltpu.get_barrier_semaphore()

    def greet(j, _):
        pl.semaphore_signal(
            barrier, inc=1, device_id=(ring, lax.rem(me + j, PEERS)), device_id_type=MESH
        )
        return 0

    for s in range(2):
        pltpu.make_async_copy(vel_hbm.at[s], vel.at[s], load_sem.at[s]).start()
    lax.fori_loop(1, PEERS, greet, 0)
    for other in (below, above):
        pl.semaphore_signal(barrier, inc=1, device_id=(other, me), device_id_type=MESH)
    v_cat[pl.ds(3 * HALF, 256 - 3 * HALF), :] = jnp.zeros((256 - 3 * HALF, 256), bf16)
    for s in range(2):
        pltpu.make_async_copy(vel_hbm.at[s], vel.at[s], load_sem.at[s]).wait()

    def spanwise(ch):
        slot = lax.rem(slot_ref[2 * ring + ch], 2)

        def residues(g, _):
            row = pl.multiple_of(g * 16, 16)
            lane = lax.broadcasted_iota(jnp.int32, (16, 128), 1)

            def tile(k):
                return vel[slot, pl.ds(row, 16), pl.ds(128 * (k % 30), 128)]

            for part in range(2):
                xs = []
                for j in range(CLASSES):
                    first, shift = divmod(SPAN * j + 128 * part, 128)
                    if shift == 0:
                        xs.append(tile(first))
                        continue
                    xs.append(
                        jnp.where(
                            lane < 128 - shift,
                            lane_roll(tile(first), 128 - shift),
                            lane_roll(tile(first + 1), 128 - shift),
                        )
                    )
                cols = pl.ds(128 * part, 128)
                cos_of = lambda c: jnp.broadcast_to(twist_ref[c, 0:1, cols], (16, 128))
                sin_of = lambda c: jnp.broadcast_to(twist_ref[c, 1:2, cols], (16, 128))
                for c, pair in enumerate(twisted_classes(xs, cos_of, sin_of)):
                    for which in range(2):
                        high, low = split(pair[which])
                        at = pl.ds(256 * which + 128 * part, 128)
                        y_hi[c, pl.ds(row, 16), at] = high
                        y_lo[c, pl.ds(row, 16), at] = low
            return 0

        lax.fori_loop(0, ROWS // 16, residues, 0)

        def products(g, _):
            high = y_hi[pl.ds(g * 4, 4)].reshape(4 * ROWS, 512)
            low = y_lo[pl.ds(g * 4, 4)].reshape(4 * ROWS, 512)
            total = jnp.dot(high, span_ref[0], preferred_element_type=f32)
            total += jnp.dot(low, span_ref[0], preferred_element_type=f32)
            total += jnp.dot(high, span_ref[1], preferred_element_type=f32)
            z_buf[pl.ds(g * 4, 4)] = total.reshape(4, ROWS, 128)
            return 0

        lax.fori_loop(0, CLASSES // 4, products, 0)

        def regroup(g, _):
            row = pl.multiple_of(g * 8, 8)
            lane = lax.broadcasted_iota(jnp.int32, (8, 128), 1)
            halves = [
                lane_exchange(
                    [z_buf[c, pl.ds(h * HALF + row, 8), :] for c in range(CLASSES)],
                    lane,
                    lane_roll,
                )
                for h in range(2)
            ]
            for tb in range(16):
                u0, u1 = halves[0][tb], halves[1][tb]
                send_buf[ch, 2 * tb, pl.ds(row, 8), :] = jnp.where(
                    lane < 64, u0, lane_roll(u1, 64)
                )
                send_buf[ch, 2 * tb + 1, pl.ds(row, 8), :] = jnp.where(
                    lane < 64, lane_roll(u0, 64), u1
                )
            return 0

        lax.fori_loop(0, HALF // 8, regroup, 0)

    def own_copy(ch):
        return pltpu.make_async_copy(
            send_buf.at[ch, me], recv_buf.at[ch, me], own_sem.at[ch]
        )

    def to_peer(ch, j):
        target = lax.rem(me + PEERS - j, PEERS)
        return pltpu.make_async_remote_copy(
            src_ref=send_buf.at[ch, target],
            dst_ref=recv_buf.at[ch, me],
            send_sem=a_send.at[ch, j],
            recv_sem=a_recv.at[ch, me],
            device_id=(ring, target),
            device_id_type=MESH,
        )

    def from_peer(ch, j):
        source = lax.rem(me + j, PEERS)
        return pltpu.make_async_remote_copy(
            src_ref=send_buf.at[ch, source],
            dst_ref=recv_buf.at[ch, source],
            send_sem=a_send.at[ch, j],
            recv_sem=a_recv.at[ch, source],
            device_id=(ring, source),
            device_id_type=MESH,
        )

    def send_all(ch):
        own_copy(ch).start()

        def one(j, _):
            to_peer(ch, j).start()
            return 0

        lax.fori_loop(1, PEERS, one, 0)

    def hop(ch, side, s):
        sign = 1 if side == 0 else -1
        return pltpu.make_async_remote_copy(
            src_ref=out_ref.at[4 + sign * (s - 1), ch],
            dst_ref=out_ref.at[4 + sign * s, ch],
            send_sem=z_send.at[ch, side, s],
            recv_sem=z_recv.at[ch, side, s],
            device_id=(below if side == 0 else above, me),
            device_id_type=MESH,
        )

    def hops_of(ch, side):
        return 4 if ch == side else 3

    def relay(ch, s):
        for side in range(2):
            if 2 <= s <= hops_of(ch, side) + 1:
                hop(ch, side, s - 1).wait_recv()
            if s <= hops_of(ch, side):
                hop(ch, side, s).start()

    def axial(ch, between):
        own_copy(ch).wait()

        def pair_step(i, _):
            @pl.when(i > 0)
            def _():
                from_peer(ch, 2 * i).wait_recv()

            from_peer(ch, 2 * i + 1).wait_recv()
            for o in range(2):
                source = lax.rem(me + 2 * i + o, PEERS)
                cols = pl.ds(128 * o, 128)
                high, low = split(recv_buf[ch, source])
                v_cat[pl.ds(0, HALF), cols] = high
                v_cat[pl.ds(HALF, HALF), cols] = low
                v_cat[pl.ds(2 * HALF, HALF), cols] = high
            q_buf[...] = jnp.dot(axial_ref[...], v_cat[...], preferred_element_type=f32)

            @pl.when(i == 0)
            def _():
                acc_a[...] = q_buf[pl.ds(0, KX), :]
                acc_b[...] = q_buf[pl.ds(KX, KX), :]

            @pl.when(i > 0)
            def _():
                cos2 = back_ref[0]
                sin2 = back_ref[1]
                for blk in range(KX // 16):
                    rows = pl.ds(16 * blk, 16)
                    a, b = acc_a[rows, :], acc_b[rows, :]
                    acc_a[rows, :] = a * cos2 + b * sin2 + q_buf[rows, :]
                    acc_b[rows, :] = b * cos2 - a * sin2 + q_buf[pl.ds(KX + 16 * blk, 16), :]

            for at, s in between:

                @pl.when(i == at)
                def _():
                    relay(0, s)

            return 0

        lax.fori_loop(0, PEERS // 2, pair_step, 0)

        k = lax.broadcasted_iota(jnp.int32, (64, 256), 0)
        lane = lax.broadcasted_iota(jnp.int32, (64, 256), 1)
        turns = lax.rem(k * (2 * (me + 30 + lane // 128) + lane // 64 % 2), 64)
        psi = turns.astype(f32) * (2.0 * math.pi / 64)
        scale = 1.0 / math.sqrt(NX * NZ)
        cos_psi = jnp.cos(psi) * scale
        sin_psi = jnp.sin(psi) * scale
        lane1 = lax.broadcasted_iota(jnp.int32, (64, 128), 1)
        for blk in range(KX // 64):
            rows = pl.ds(64 * blk, 64)
            a, b = acc_a[rows, :], acc_b[rows, :]
            pr = a * cos_psi - b * sin_psi
            qr = a * sin_psi + b * cos_psi
            pr = pr[:, :128] + pr[:, 128:]
            qr = qr[:, :128] + qr[:, 128:]
            pr = pr + lane_roll(pr, 64)
            qr = qr + lane_roll(qr, 64)
            turned = lane_roll(qr, 32)
            s_rows = pr + jnp.where(lane1 // 32 % 2 == 0, turned, -turned)
            q_buf[rows, pl.ds(0, 128)] = s_rows
        for blk in range(KX // 128):
            block = q_buf[pl.ds(128 * blk, 128), pl.ds(0, 128)]
            out_ref[4, ch, :, pl.ds(128 * blk, 128)] = block.T[:64, :]

    spanwise(0)
    pl.semaphore_wait(barrier, PEERS + 1)
    send_all(0)
    spanwise(1)
    send_all(1)
    axial(0, ())
    relay(0, 1)
    axial(1, ((4, 2), (8, 3), (12, 4)))
    relay(1, 1)
    relay(0, 5)
    for s in range(2, 6):
        relay(1, s)
    for ch in range(2):

        def sent(j, _):
            to_peer(ch, j).wait_send()
            return 0

        lax.fori_loop(1, PEERS, sent, 0)
        for side in range(2):
            for s in range(1, hops_of(ch, side) + 1):
                hop(ch, side, s).wait_send()


def cross_kernel(flag_ref, spec_ref, band_ref, partner_ref):
    ring = lax.axis_index("plane")
    own = pl.program_id(0)
    for i in range(2):

        @pl.when(own == i)
        def _():
            def pair(kz, _):
                row = pl.multiple_of(kz * 8, 8)
                re0 = spec_ref[4, i, pl.ds(row, 8), :]
                im0 = spec_ref[4, i, pl.ds(32 + row, 8), :]
                for out, sign in ((band_ref, 1), (partner_ref, -1)):
                    for d in range(BAND):
                        off, odd = divmod(i + sign * d, 2)
                        re1 = spec_ref[4 + off, odd, pl.ds(row, 8), :]
                        im1 = spec_ref[4 + off, odd, pl.ds(32 + row, 8), :]
                        which = 0 if sign == 1 else 1
                        ask = flag_ref[which, i * BAND + d] != 0
                        out[0, d, 0, pl.ds(row, 8), :] = jnp.where(
                            ask, re0 * re1 + im0 * im1, 0.0
                        )
                        out[0, d, 1, pl.ds(row, 8), :] = jnp.where(
                            ask, im0 * re1 - re0 * im1, 0.0
                        )
                return 0

            lax.fori_loop(0, 4, pair, 0)


def local(velocity, plane_slot, pair_list):
    span, twist, axial_cat, back = [jnp.asarray(t) for t in tables()]
    vmem = pl.BlockSpec(memory_space=pltpu.VMEM)
    spectra = pl.pallas_call(
        transform_kernel,
        out_shape=jax.ShapeDtypeStruct((9, 2, 64, KX), f32),
        in_specs=[
            pl.BlockSpec(memory_space=pltpu.SMEM),
            pl.BlockSpec(memory_space=pl.ANY),
            vmem,
            vmem,
            vmem,
            vmem,
        ],
        out_specs=vmem,
        scratch_shapes=[
            pltpu.VMEM((2, ROWS, NZ), f32),
            pltpu.VMEM((CLASSES, ROWS, 512), bf16),
            pltpu.VMEM((CLASSES, ROWS, 512), bf16),
            pltpu.VMEM((CLASSES, ROWS, 128), f32),
            pltpu.VMEM((2, PEERS, HALF, 128), f32),
            pltpu.VMEM((2, PEERS, HALF, 128), f32),
            pltpu.VMEM((256, 256), bf16),
            pltpu.VMEM((2 * KX, 256), f32),
            pltpu.VMEM((KX, 256), f32),
            pltpu.VMEM((KX, 256), f32),
            pltpu.SemaphoreType.DMA((2,)),
            pltpu.SemaphoreType.DMA((2,)),
            pltpu.SemaphoreType.DMA((2, PEERS)),
            pltpu.SemaphoreType.DMA((2, PEERS)),
            pltpu.SemaphoreType.DMA((2, 2, 5)),
            pltpu.SemaphoreType.DMA((2, 2, 5)),
        ],
        compiler_params=pltpu.CompilerParams(collective_id=0, has_side_effects=True),
        name="transform",
    )(plane_slot, velocity, span, twist, axial_cat, back)

    first_plane = lax.axis_index("plane") * 2
    code = pair_list[:, 0] * BAND + pair_list[:, 1] - pair_list[:, 0]
    own = first_plane + lax.broadcasted_iota(jnp.int32, (2, BAND), 0)
    gap = lax.broadcasted_iota(jnp.int32, (2, BAND), 1)
    up = own * BAND + gap
    down = jnp.where(own >= gap, (own - gap) * BAND + gap, -1)
    asked = jnp.stack([up, down]).reshape(2, 2 * BAND, 1)
    flags = jnp.any(asked == code, axis=2).astype(jnp.int32)

    share = KZ // PEERS
    out = jax.ShapeDtypeStruct((2, BAND, 2, share, KX), f32)
    block = pl.BlockSpec((1, BAND, 2, share, KX), lambda i: (i, 0, 0, 0, 0))
    band_cross, partner_cross = pl.pallas_call(
        cross_kernel,
        grid=(2,),
        out_shape=(out, out),
        in_specs=[
            pl.BlockSpec(memory_space=pltpu.SMEM),
            pl.BlockSpec((9, 2, 64, KX), lambda i: (0, 0, 0, 0)),
        ],
        out_specs=(block, block),
        name="cross",
    )(flags, spectra)
    return (band_cross, partner_cross)


def solution(mesh):
    return jax.shard_map(
        local,
        mesh=mesh,
        in_specs=(P("plane", "pencil", None), P(), P()),
        out_specs=(P("plane", None, None, "pencil", None), P("plane", None, None, "pencil", None)),
        check_vma=False,
    )
```

profile of v0, /device:TPU:32, one launch (start us, length us, event | category | flops | bytes accessed | tf_op | source)
XLA Modules:
  0.0 95.5 jit_solution(12979514270075742143)
XLA Ops:
  0.6 0.8 fusion
  1.4 0.1 iota.36
  1.5 0.1 iota.37
  1.6 0.1 iota.32
  1.6 0.1 iota.33
  1.7 0.1 iota.35
  1.8 0.2 compare_reduce_fusion
  2.0 0.5 convert_element_type.3.flag_ref
  2.5 89.0 %transform.1.spec_ref = f32[9,2,64,512]{3,2,1,0:T(8,128)} custom-call(s32[16]{0:T(128)} %slot_ref.1, f32[2,160,3840]{2,1,0:T(8,128)} %vel_hbm.1, bf16[2,512,128]{2,1,0:T(8,128)(2,1)} %constant.23.clone.span_ref, f32[16,2,256]{2,1,0:T(2,128)} %constant.24.clone.twist_ref, bf16[1024,256]{1,0:T(8,128)(2,1)} %constant.25.clone.axial_ref, ...), custom_call_target="tpu_custom_call" | custom-call | tf_op jit(solution)/shard_map/transform/pallas_call | solution.py:433
  91.5 4.0 %cross.1 = (f32[2,8,2,32,512]{4,3,2,1,0:T(8,128)}, f32[2,8,2,32,512]{4,3,2,1,0:T(8,128)}) custom-call(s32[2,16]{1,0:T(2,128)} %convert_element_type.3.flag_ref, f32[9,2,64,512]{3,2,1,0:T(8,128)} %transform.1.spec_ref), custom_call_target="tpu_custom_call" | custom-call | tf_op jit(solution)/shard_map/cross/pallas_call | solution.py:479
  (4 shorter events, 0.0 us)
where the time goes:
time: 95.7 us; the launch traced here: 95.5 us
  Pallas kernels  93 us (97%)
  other arithmetic  1.49 us (2%)
    pallas_call x1, Pallas kernels, local(): pl.pallas_call(transform_kernel, out_shape=jax.ShapeDtypeStruct((9, 2, 64...  89 us
    pallas_call x1, Pallas kernels, local(): pl.pallas_call(cross_kernel, grid=(2,), out_shape=(out, out), in_specs=[p...  4.01 us

commit v1 on v0

v1 whole, which is shorter than its diff:
```python
import functools
import math

import jax
import jax.numpy as jnp
import numpy as np
from jax import lax
from jax.experimental import pallas as pl
from jax.experimental.pallas import tpu as pltpu
from jax.sharding import PartitionSpec as P

NX = 5120
NZ = 3840
KX = 512
KZ = 1024
BAND = 8
CLASSES = 16
SPAN = NZ // CLASSES
PEERS = 32
RINGS = 8
ROWS = NX // PEERS
DEPTH = 1024
MESH = pl.DeviceIdType.MESH
bf16 = jnp.bfloat16
f32 = jnp.float32


def split_np(table):
    high = np.asarray(table, np.float32).astype(bf16)
    low = (table - high.astype(np.float64)).astype(np.float32).astype(bf16)
    return high, low


@functools.cache
def tables():
    lane = np.arange(128)
    route, other, ri = lane // 8, lane // 2 % 4, lane % 2
    first, group, core = route // 8, route // 2 % 4, route % 2
    x_at = np.where(first == 0, other, group)
    y_at = np.where(first == 0, group, other)
    m = 2 * (x_at * 8 + y_at * 2 + core) + first
    z = np.arange(256)
    phase = 2 * np.pi * ((z[:, None] * m[None, :]) % SPAN) / SPAN
    real_rows = np.where(ri == 0, np.cos(phase), -np.sin(phase))
    imag_rows = np.where(ri == 0, np.sin(phase), np.cos(phase))
    inside = (z < SPAN)[:, None]
    span = np.concatenate([real_rows * inside, imag_rows * inside], axis=0)

    c = np.arange(CLASSES)
    turn = 2 * np.pi * (c[:, None] * z[None, :]) / NZ
    keep = (z < SPAN)[None, :]
    twist = np.stack([np.cos(turn) * keep, np.sin(turn) * keep], axis=1).astype(np.float32)

    k = np.arange(KX)
    kx = np.where(k < KX // 2, k, k - KX)
    r = np.arange(2 * ROWS)
    theta = 2 * np.pi * ((kx[:, None] * r[None, :]) % NX) / NX
    ax_hi, ax_lo = split_np(np.concatenate([np.cos(theta), np.sin(theta)], axis=0))
    parts = []
    for core in range(2):
        rows = slice(core * ROWS, core * ROWS + ROWS)
        parts += [ax_hi[:, rows], ax_hi[:, rows], ax_lo[:, rows]]
    parts.append(np.zeros((2 * KX, DEPTH - 6 * ROWS), bf16))
    return np.stack(split_np(span)), twist, np.concatenate(parts, axis=1)


def times(a, w):
    ar, ai = a
    wr, wi = w
    s = math.sqrt(0.5)
    if abs(wr - 1) < 1e-12:
        return a
    if abs(wr) < 1e-12 and abs(wi + 1) < 1e-12:
        return (ai, None if ar is None else -ar)
    if abs(wr - s) < 1e-12 and abs(wi + s) < 1e-12 and ai is not None:
        return ((ar + ai) * s, (ai - ar) * s)
    if ai is None:
        return (ar * wr, ar * wi)
    return (ar * wr - ai * wi, ar * wi + ai * wr)


def add(a, b):
    if a is None:
        return b
    if b is None:
        return a
    return a + b


def sub(a, b):
    if b is None:
        return a
    if a is None:
        return -b
    return a - b


def real_fft(xs):
    n = len(xs)
    if n == 1:
        return [(xs[0], None)]
    even = real_fft(xs[0::2])
    odd = real_fft(xs[1::2])
    out = [None] * (n // 2 + 1)
    for k in range(n // 4 + 1):
        w = (math.cos(2 * math.pi * k / n), -math.sin(2 * math.pi * k / n))
        er, ei = even[k]
        tr, ti = times(odd[k], w)
        out[k] = (add(er, tr), add(ei, ti))
        if n // 2 - k != k:
            out[n // 2 - k] = (sub(er, tr), sub(ti, ei))
    return out


def twisted_classes(xs, cos_of, sin_of):
    modes = real_fft(xs)
    out = []
    for c in range(CLASSES):
        a, b = modes[c] if c <= 8 else modes[16 - c]
        if c == 0:
            out.append((a, jnp.zeros_like(a)))
            continue
        tc, ts = cos_of(c), sin_of(c)
        if b is None:
            out.append((a * tc, -(a * ts)))
        elif c < 8:
            out.append((a * tc + b * ts, b * tc - a * ts))
        else:
            out.append((a * tc - b * ts, -(b * tc + a * ts)))
    return out


def split(x):
    high = x.astype(bf16)
    return high, (x - high.astype(f32)).astype(bf16)


def lane_exchange(tiles, lane, roll):
    turned = [t if c == 0 else roll(t, 8 * c) for c, t in enumerate(tiles)]
    tiles = [turned[-j % 16] for j in range(16)]
    for bit in range(4):
        gap = 1 << bit
        high_block = (lane & (8 * gap)) != 0
        tiles = [jnp.where(high_block, tiles[j - gap], tiles[j]) for j in range(16)]
    return tiles


def lane_roll(x, shift):
    return pltpu.roll(x, shift, 1)


def transform_kernel(
    slot_ref, vel_hbm, span_ref, twist_ref, axial_hbm, out_ref,
    vel, axial_ref, y_hi, y_lo, z_buf, send_buf, recv_buf, v_cat, q_buf, turn_buf,
    flip_buf, part_buf, sum_buf, load_sem, table_sem, own_sem, a_send, a_recv, b_send, b_recv,
    z_send, z_recv,
):
    me = lax.axis_index("pencil")
    ring = lax.axis_index("plane")
    below = lax.rem(ring + RINGS - 1, RINGS)
    above = lax.rem(ring + 1, RINGS)
    core = lax.rem(me, 2)
    y_at = lax.rem(me // 2, 4)
    x_at = me // 8
    place = (y_at, x_at)
    across = (x_at, y_at)

    def member(half, group, core_at):
        if half == 0:
            return x_at * 8 + group * 2 + core_at
        return group * 8 + y_at * 2 + core_at

    barrier = pltpu.get_barrier_semaphore()

    def load(slot, part):
        rows = pl.ds(part * 32, 32)
        return pltpu.make_async_copy(
            vel_hbm.at[slot, rows], vel.at[slot, rows], load_sem.at[slot, part]
        )

    for part in range(ROWS // 32):
        for slot in range(2):
            load(slot, part).start()
    tables_in = pltpu.make_async_copy(axial_hbm, axial_ref, table_sem)
    tables_in.start()
    for half in range(2):
        for step in range(4):
            for flip in range(2):
                if step == 0 and (flip == 0 or half == 1):
                    continue
                peer = member(half, lax.rem(place[half] + step, 4), lax.rem(core + flip, 2))
                pl.semaphore_signal(barrier, inc=1, device_id=(ring, peer), device_id_type=MESH)
    for other in (below, above):
        pl.semaphore_signal(barrier, inc=1, device_id=(other, me), device_id_type=MESH)
    v_cat[pl.ds(6 * ROWS, DEPTH - 6 * ROWS), :] = jnp.zeros((DEPTH - 6 * ROWS, 256), bf16)

    def spanwise(ch):
        slot = lax.rem(slot_ref[2 * ring + ch], 2)

        def residues(g, _):
            row = pl.multiple_of(g * 16, 16)
            lane = lax.broadcasted_iota(jnp.int32, (16, 128), 1)
            if ch == 0:

                @pl.when(lax.rem(g, 2) == 0)
                def _():
                    for s in range(2):
                        load(s, g // 2).wait()

            def tile(k):
                at = (pl.ds(row, 16), pl.ds(128 * (k % 30), 128))
                return jnp.where(slot == 0, vel[(0,) + at], vel[(1,) + at])

            for part in range(2):
                xs = []
                for j in range(CLASSES):
                    first, shift = divmod(SPAN * j + 128 * part, 128)
                    if shift == 0:
                        xs.append(tile(first))
                        continue
                    xs.append(
                        jnp.where(
                            lane < 128 - shift,
                            lane_roll(tile(first), 128 - shift),
                            lane_roll(tile(first + 1), 128 - shift),
                        )
                    )
                cols = pl.ds(128 * part, 128)
                cos_of = lambda c: jnp.broadcast_to(twist_ref[c, 0:1, cols], (16, 128))
                sin_of = lambda c: jnp.broadcast_to(twist_ref[c, 1:2, cols], (16, 128))
                for c, pair in enumerate(twisted_classes(xs, cos_of, sin_of)):
                    for which in range(2):
                        high, low = split(pair[which])
                        at = pl.ds(256 * which + 128 * part, 128)
                        y_hi[c, pl.ds(row, 16), at] = high
                        y_lo[c, pl.ds(row, 16), at] = low
            return 0

        lax.fori_loop(0, ROWS // 16, residues, 0)

        def products(g, _):
            high = y_hi[pl.ds(g * 4, 4)].reshape(4 * ROWS, 512)
            low = y_lo[pl.ds(g * 4, 4)].reshape(4 * ROWS, 512)
            total = jnp.dot(high, span_ref[0], preferred_element_type=f32)
            total += jnp.dot(low, span_ref[0], preferred_element_type=f32)
            total += jnp.dot(high, span_ref[1], preferred_element_type=f32)
            z_buf[pl.ds(g * 4, 4)] = total.reshape(4, ROWS, 128)
            return 0

        lax.fori_loop(0, CLASSES // 4, products, 0)

        def regroup(g, _):
            lane = lax.broadcasted_iota(jnp.int32, (8, 128), 1)
            for part in range(2):
                row = pl.multiple_of(g * 16 + part * 8, 8)
                tiles = [z_buf[c, pl.ds(row, 8), :] for c in range(CLASSES)]
                for f, tile in enumerate(lane_exchange(tiles, lane, lane_roll)):
                    send_buf[ch, f, pl.ds(row, 8), :] = tile
            return 0

        lax.fori_loop(0, ROWS // 16, regroup, 0)

    def own_copy(ch, half):
        mine = place[half] * 2 + core
        return pltpu.make_async_copy(
            send_buf.at[ch, 8 * half + mine], recv_buf.at[ch, half, mine], own_sem.at[ch, half]
        )

    def first_hop(ch, half, step, flip, back=False):
        mine = place[half] * 2 + core
        group = lax.rem(place[half] + step, 4)
        core_at = lax.rem(core + flip, 2)
        peer = group * 2 + core_at
        return pltpu.make_async_remote_copy(
            src_ref=send_buf.at[ch, 8 * half + peer],
            dst_ref=recv_buf.at[ch, half, peer if back else mine],
            send_sem=a_send.at[ch, half, 2 * step + flip],
            recv_sem=a_recv.at[ch, half, peer if back else mine],
            device_id=(ring, member(half, group, core_at)),
            device_id_type=MESH,
        )

    def second_hop(ch, half, step, back=False):
        there = lax.rem(across[half] + step, 4)
        return pltpu.make_async_remote_copy(
            src_ref=part_buf.at[ch, half, there],
            dst_ref=sum_buf.at[ch, half, there if back else across[half]],
            send_sem=b_send.at[ch, half, step],
            recv_sem=b_recv.at[ch, half, there if back else across[half]],
            device_id=(ring, member(1 - half, there, core)),
            device_id_type=MESH,
        )

    first_order = ((1, 0), (3, 0), (1, 1), (3, 1), (2, 0), (2, 1), (0, 1))

    def send_all(ch):
        for half in range(2):
            own_copy(ch, half).start()
        for step, flip in first_order:
            for half in range(2):
                first_hop(ch, half, step, flip).start()

    def hop(ch, half, side, s):
        sign = 1 if side == 0 else -1
        return pltpu.make_async_remote_copy(
            src_ref=out_ref.at[4 + sign * (s - 1), ch, half],
            dst_ref=out_ref.at[4 + sign * s, ch, half],
            send_sem=z_send.at[ch, half, side, s],
            recv_sem=z_recv.at[ch, half, side, s],
            device_id=(below if side == 0 else above, me),
            device_id_type=MESH,
        )

    def hops_of(ch, side):
        return 4 if ch == side else 3

    def relay(ch, half, s):
        for side in range(2):
            if 2 <= s <= hops_of(ch, side) + 1:
                hop(ch, half, side, s - 1).wait_recv()
            if s <= hops_of(ch, side):
                hop(ch, half, side, s).start()

    def axial(ch, half):
        own_copy(ch, half).wait()
        for step, flip in first_order:
            first_hop(ch, half, step, flip, back=True).wait_recv()

        def pair_step(s, _):
            for o in range(2):
                cols = pl.ds(128 * o, 128)
                for c in range(2):
                    high, low = split(recv_buf[ch, half, 4 * s + 2 * o + c])
                    v_cat[pl.ds(3 * c * ROWS, ROWS), cols] = high
                    v_cat[pl.ds((3 * c + 1) * ROWS, ROWS), cols] = low
                    v_cat[pl.ds((3 * c + 2) * ROWS, ROWS), cols] = high
            q_buf[s] = jnp.dot(axial_ref[...], v_cat[...], preferred_element_type=f32)
            return 0

        lax.fori_loop(0, 2, pair_step, 0)

        k = lax.broadcasted_iota(jnp.int32, (16, 256), 0)
        o = lax.broadcasted_iota(jnp.int32, (16, 256), 1) // 128
        scale = 1.0 / math.sqrt(NX * NZ)
        cos_of, sin_of = [], []
        for s in range(2):
            group = 2 * s + o
            steps = 4 * x_at + group if half == 0 else 4 * group + y_at
            psi = lax.rem(k * steps, 16).astype(f32) * (2.0 * math.pi / 16)
            cos_of.append(jnp.cos(psi) * scale)
            sin_of.append(jnp.sin(psi) * scale)
        lane = lax.broadcasted_iota(jnp.int32, (16, 128), 1)
        even = lane % 2 == 0
        mine = 8 * half + place[half] * 2 + core
        shift = lax.rem(128 - 8 * mine, 128)
        for blk in range(KX // 16):
            p = q = 0.0
            for s in range(2):
                a = q_buf[s, pl.ds(16 * blk, 16), :]
                b = q_buf[s, pl.ds(KX + 16 * blk, 16), :]
                p = p + (a * cos_of[s] - b * sin_of[s])
                q = q + (a * sin_of[s] + b * cos_of[s])
            p = p[:, :128] + p[:, 128:]
            q = q[:, :128] + q[:, 128:]
            q = jnp.where(even, -q, q)
            turn_buf[0, pl.ds(16 * blk, 16), :] = lane_roll(p, shift)
            turn_buf[1, pl.ds(16 * blk, 16), :] = lane_roll(q, shift)
        for blk in range(KX // 128):
            rows = pl.ds(128 * blk, 128)
            for which in range(2):
                flip_buf[which, blk] = turn_buf[which, rows, :].T
            for there in range(4):
                for ri in range(2):
                    straight = flip_buf[0, blk, pl.ds(2 * there + ri, 16, stride=8), :]
                    crossed = flip_buf[1, blk, pl.ds(2 * there + 1 - ri, 16, stride=8), :]
                    part_buf[ch, half, there, ri, :, rows] = straight + crossed
        for step in (1, 3, 2):
            second_hop(ch, half, step).start()

    def gather(ch, half):
        total = part_buf[ch, half, across[half]]
        for step in (1, 3, 2):
            second_hop(ch, half, step, back=True).wait_recv()
        for step in range(1, 4):
            total = total + sum_buf[ch, half, lax.rem(across[half] + step, 4)]
        out_ref[4, ch, half] = total
        relay(ch, half, 1)

    spanwise(0)
    pl.semaphore_wait(barrier, 15)
    send_all(0)
    spanwise(1)
    send_all(1)
    tables_in.wait()
    axial(0, 0)
    axial(0, 1)
    gather(0, 0)
    gather(0, 1)
    axial(1, 0)
    relay(0, 0, 2)
    relay(0, 1, 2)
    axial(1, 1)
    relay(0, 0, 3)
    relay(0, 1, 3)
    gather(1, 0)
    gather(1, 1)
    relay(0, 0, 4)
    relay(0, 1, 4)
    for s in range(2, 6):
        if s == 3:
            relay(0, 0, 5)
            relay(0, 1, 5)
        relay(1, 0, s)
        relay(1, 1, s)
    for ch in range(2):
        for half in range(2):
            for step, flip in first_order:
                first_hop(ch, half, step, flip).wait_send()
            for step in (1, 3, 2):
                second_hop(ch, half, step).wait_send()
            for side in range(2):
                for s in range(1, hops_of(ch, side) + 1):
                    hop(ch, half, side, s).wait_send()


def cross_kernel(flag_ref, spec_ref, band_ref, partner_ref):
    ring = lax.axis_index("plane")
    own = pl.program_id(0)
    for i in range(2):

        @pl.when(own == i)
        def _():
            def pair(g, _):
                half = g // 2
                row = pl.multiple_of(lax.rem(g, 2) * 8, 8)
                at = pl.multiple_of(g * 8, 8)
                re0 = spec_ref[4, i, half, 0, pl.ds(row, 8), :]
                im0 = spec_ref[4, i, half, 1, pl.ds(row, 8), :]
                for out, sign in ((band_ref, 1), (partner_ref, -1)):
                    for d in range(BAND):
                        off, odd = divmod(i + sign * d, 2)
                        re1 = spec_ref[4 + off, odd, half, 0, pl.ds(row, 8), :]
                        im1 = spec_ref[4 + off, odd, half, 1, pl.ds(row, 8), :]
                        which = 0 if sign == 1 else 1
                        ask = flag_ref[which, i * BAND + d] != 0
                        out[0, d, 0, pl.ds(at, 8), :] = jnp.where(ask, re0 * re1 + im0 * im1, 0.0)
                        out[0, d, 1, pl.ds(at, 8), :] = jnp.where(ask, im0 * re1 - re0 * im1, 0.0)
                return 0

            lax.fori_loop(0, 4, pair, 0)


def local(velocity, plane_slot, pair_list):
    span, twist, axial_cat = [jnp.asarray(t) for t in tables()]
    vmem = pl.BlockSpec(memory_space=pltpu.VMEM)
    anywhere = pl.BlockSpec(memory_space=pl.ANY)
    slab = (2, 2, 2, 16, KX)
    dma = pltpu.SemaphoreType.DMA
    spectra = pl.pallas_call(
        transform_kernel,
        out_shape=jax.ShapeDtypeStruct((9,) + slab, f32),
        in_specs=[pl.BlockSpec(memory_space=pltpu.SMEM), anywhere, vmem, vmem, anywhere],
        out_specs=vmem,
        scratch_shapes=[
            pltpu.VMEM((2, ROWS, NZ), f32),
            pltpu.VMEM((2 * KX, DEPTH), bf16),
            pltpu.VMEM((CLASSES, ROWS, 512), bf16),
            pltpu.VMEM((CLASSES, ROWS, 512), bf16),
            pltpu.VMEM((CLASSES, ROWS, 128), f32),
            pltpu.VMEM((2, CLASSES, ROWS, 128), f32),
            pltpu.VMEM((2, 2, 8, ROWS, 128), f32),
            pltpu.VMEM((DEPTH, 256), bf16),
            pltpu.VMEM((2, 2 * KX, 256), f32),
            pltpu.VMEM((2, KX, 128), f32),
            pltpu.VMEM((2, KX // 128, 128, 128), f32),
            pltpu.VMEM((2, 2, 4, 2, 16, KX), f32),
            pltpu.VMEM((2, 2, 4, 2, 16, KX), f32),
            dma((2, ROWS // 32)),
            dma,
            dma((2, 2)),
            dma((2, 2, 8)),
            dma((2, 2, 8)),
            dma((2, 2, 4)),
            dma((2, 2, 4)),
            dma((2, 2, 2, 5)),
            dma((2, 2, 2, 5)),
        ],
        compiler_params=pltpu.CompilerParams(collective_id=0, has_side_effects=True),
        name="transform",
    )(plane_slot, velocity, span, twist, axial_cat)

    first_plane = lax.axis_index("plane") * 2
    code = pair_list[:, 0] * BAND + pair_list[:, 1] - pair_list[:, 0]
    own = first_plane + lax.broadcasted_iota(jnp.int32, (2, BAND), 0)
    gap = lax.broadcasted_iota(jnp.int32, (2, BAND), 1)
    up = own * BAND + gap
    down = jnp.where(own >= gap, (own - gap) * BAND + gap, -1)
    asked = jnp.stack([up, down]).reshape(2, 2 * BAND, 1)
    flags = jnp.any(asked == code, axis=2).astype(jnp.int32)

    share = KZ // PEERS
    out = jax.ShapeDtypeStruct((2, BAND, 2, share, KX), f32)
    block = pl.BlockSpec((1, BAND, 2, share, KX), lambda i: (i, 0, 0, 0, 0))
    band_cross, partner_cross = pl.pallas_call(
        cross_kernel,
        grid=(2,),
        out_shape=(out, out),
        in_specs=[
            pl.BlockSpec(memory_space=pltpu.SMEM),
            pl.BlockSpec((9,) + slab, lambda i: (0,) * 6),
        ],
        out_specs=(block, block),
        name="cross",
    )(flags, spectra)
    return (band_cross, partner_cross)


def solution(mesh):
    return jax.shard_map(
        local,
        mesh=mesh,
        in_specs=(P("plane", "pencil", None), P(), P()),
        out_specs=(P("plane", None, None, "pencil", None), P("plane", None, None, "pencil", None)),
        check_vma=False,
    )
```

time: 95.7 us -> 72.5 us (0.76)
  the two profiles are of different devices: /device:TPU:32 before, /device:TPU:2 now
where the time goes in v1:
time: 72.5 us; the launch traced here: 72.2 us
  Pallas kernels  69.7 us (96%)
  other arithmetic  1.49 us (2%)
    pallas_call x1, Pallas kernels, local(): pl.pallas_call(transform_kernel, out_shape=jax.ShapeDtypeStruct((9,) + sl...  65.7 us
    pallas_call x1, Pallas kernels, local(): pl.pallas_call(cross_kernel, grid=(2,), out_shape=(out, out), in_specs=[p...  4.04 us

profile of v1, /device:TPU:2, one launch (start us, length us, event | category | flops | bytes accessed | tf_op | source)
XLA Modules:
  0.0 72.2 jit_solution(2281411821864178115)
XLA Ops:
  0.6 0.8 %fusion = s32[80]{0:T(128)S(1)} fusion(s32[80,2]{0,1:T(2,128)} %param.8), kind=kLoop, calls=%fused_computation.4 | loop fusion | flops 240 | bytes 960 | tf_op jit(solution)/shard_map/sub | solution.py:493
  1.4 0.1 iota.36
  1.5 0.1 iota.37
  1.6 0.1 iota.32
  1.6 0.1 iota.33
  1.7 0.1 iota.35
  1.8 0.2 compare_reduce_fusion
  2.0 0.5 convert_element_type.3.flag_ref
  2.5 65.7 %transform.1.spec_ref = f32[9,2,2,2,16,512]{5,4,3,2,1,0:T(8,128)} custom-call(s32[16]{0:T(128)} %slot_ref.1, f32[2,160,3840]{2,1,0:T(8,128)} %vel_hbm.1, bf16[2,512,128]{2,1,0:T(8,128)(2,1)} %constant.21.clone.span_ref, f32[16,2,256]{2,1,0:T(2,128)} %constant.22.clone.twist_ref, bf16[1024,1024]{1,0:T(8,128)(2,1)} %constant.23.clone.axial_hbm), custom_call_target="tpu_custom_call" | custom-call | tf_op jit(solution)/shard_map/transform/pallas_call | solution.py:459
  68.2 4.0 %cross.1 = (f32[2,8,2,32,512]{4,3,2,1,0:T(8,128)}, f32[2,8,2,32,512]{4,3,2,1,0:T(8,128)}) custom-call(s32[2,16]{1,0:T(2,128)} %convert_element_type.3.flag_ref, f32[9,2,2,2,16,512]{5,4,3,2,1,0:T(8,128)} %transform.1.spec_ref), custom_call_target="tpu_custom_call" | custom-call | tf_op jit(solution)/shard_map/cross/pallas_call | solution.py:504
  (4 shorter events, 0.0 us)

commit v2 on v1

--- a/solution.py
+++ b/solution.py
@@ -151,7 +151,7 @@
 
 def transform_kernel(
     slot_ref, vel_hbm, span_ref, twist_ref, axial_hbm, out_ref,
-    vel, axial_ref, y_hi, y_lo, z_buf, send_buf, recv_buf, v_cat, q_buf, turn_buf,
+    vel, axial_ref, hi_even, lo_even, hi_odd, lo_odd, z_even, z_odd, send_buf, recv_buf, v_cat, q_buf, turn_buf,
     flip_buf, part_buf, sum_buf, load_sem, table_sem, own_sem, a_send, a_recv, b_send, b_recv,
     z_send, z_recv,
 ):
@@ -194,71 +194,57 @@
         pl.semaphore_signal(barrier, inc=1, device_id=(other, me), device_id_type=MESH)
     v_cat[pl.ds(6 * ROWS, DEPTH - 6 * ROWS), :] = jnp.zeros((DEPTH - 6 * ROWS, 256), bf16)
 
-    def spanwise(ch):
-        slot = lax.rem(slot_ref[2 * ring + ch], 2)
-
-        def residues(g, _):
-            row = pl.multiple_of(g * 16, 16)
-            lane = lax.broadcasted_iota(jnp.int32, (16, 128), 1)
-            if ch == 0:
-
-                @pl.when(lax.rem(g, 2) == 0)
-                def _():
-                    for s in range(2):
-                        load(s, g // 2).wait()
-
-            def tile(k):
-                at = (pl.ds(row, 16), pl.ds(128 * (k % 30), 128))
-                return jnp.where(slot == 0, vel[(0,) + at], vel[(1,) + at])
-
-            for part in range(2):
-                xs = []
-                for j in range(CLASSES):
-                    first, shift = divmod(SPAN * j + 128 * part, 128)
-                    if shift == 0:
-                        xs.append(tile(first))
-                        continue
-                    xs.append(
-                        jnp.where(
-                            lane < 128 - shift,
-                            lane_roll(tile(first), 128 - shift),
-                            lane_roll(tile(first + 1), 128 - shift),
-                        )
+    lane16 = lax.broadcasted_iota(jnp.int32, (16, 128), 1)
+    lane8 = lax.broadcasted_iota(jnp.int32, (8, 128), 1)
+    groups = ROWS // 16
+
+    def residues(g, y_hi, y_lo):
+        slot = lax.rem(slot_ref[2 * ring + g // groups], 2)
+        row = pl.multiple_of(lax.rem(g, groups) * 16, 16)
+
+        def tile(k):
+            at = (pl.ds(row, 16), pl.ds(128 * (k % 30), 128))
+            return jnp.where(slot == 0, vel[(0,) + at], vel[(1,) + at])
+
+        for part in range(2):
+            xs = []
+            for j in range(CLASSES):
+                first, shift = divmod(SPAN * j + 128 * part, 128)
+                if shift == 0:
+                    xs.append(tile(first))
+                    continue
+                xs.append(
+                    jnp.where(
+                        lane16 < 128 - shift,
+                        lane_roll(tile(first), 128 - shift),
+                        lane_roll(tile(first + 1), 128 - shift),
                     )
-                cols = pl.ds(128 * part, 128)
-                cos_of = lambda c: jnp.broadcast_to(twist_ref[c, 0:1, cols], (16, 128))
-                sin_of = lambda c: jnp.broadcast_to(twist_ref[c, 1:2, cols], (16, 128))
-                for c, pair in enumerate(twisted_classes(xs, cos_of, sin_of)):
-                    for which in range(2):
-                        high, low = split(pair[which])
-                        at = pl.ds(256 * which + 128 * part, 128)
-                        y_hi[c, pl.ds(row, 16), at] = high
-                        y_lo[c, pl.ds(row, 16), at] = low
-            return 0
-
-        lax.fori_loop(0, ROWS // 16, residues, 0)
-
-        def products(g, _):
-            high = y_hi[pl.ds(g * 4, 4)].reshape(4 * ROWS, 512)
-            low = y_lo[pl.ds(g * 4, 4)].reshape(4 * ROWS, 512)
-            total = jnp.dot(high, span_ref[0], preferred_element_type=f32)
-            total += jnp.dot(low, span_ref[0], preferred_element_type=f32)
-            total += jnp.dot(high, span_ref[1], preferred_element_type=f32)
-            z_buf[pl.ds(g * 4, 4)] = total.reshape(4, ROWS, 128)
-            return 0
-
-        lax.fori_loop(0, CLASSES // 4, products, 0)
-
-        def regroup(g, _):
-            lane = lax.broadcasted_iota(jnp.int32, (8, 128), 1)
-            for part in range(2):
-                row = pl.multiple_of(g * 16 + part * 8, 8)
-                tiles = [z_buf[c, pl.ds(row, 8), :] for c in range(CLASSES)]
-                for f, tile in enumerate(lane_exchange(tiles, lane, lane_roll)):
-                    send_buf[ch, f, pl.ds(row, 8), :] = tile
-            return 0
-
-        lax.fori_loop(0, ROWS // 16, regroup, 0)
+                )
+            cols = pl.ds(128 * part, 128)
+            cos_of = lambda c: jnp.broadcast_to(twist_ref[c, 0:1, cols], (16, 128))
+            sin_of = lambda c: jnp.broadcast_to(twist_ref[c, 1:2, cols], (16, 128))
+            for c, pair in enumerate(twisted_classes(xs, cos_of, sin_of)):
+                for which in range(2):
+                    high, low = split(pair[which])
+                    at = pl.ds(256 * which + 128 * part, 128)
+                    y_hi[c, :, at] = high
+                    y_lo[c, :, at] = low
+
+    def products(y_hi, y_lo, z_buf):
+        high = y_hi[...].reshape(CLASSES * 16, 512)
+        low = y_lo[...].reshape(CLASSES * 16, 512)
+        total = jnp.dot(high, span_ref[0], preferred_element_type=f32)
+        total += jnp.dot(low, span_ref[0], preferred_element_type=f32)
+        total += jnp.dot(high, span_ref[1], preferred_element_type=f32)
+        z_buf[...] = total.reshape(CLASSES, 16, 128)
+
+    def regroup(g, z_buf):
+        g = jnp.maximum(g, 0)
+        row = pl.multiple_of(lax.rem(g, groups) * 16, 16)
+        for part in range(2):
+            tiles = [z_buf[c, pl.ds(8 * part, 8), :] for c in range(CLASSES)]
+            for f, tile in enumerate(lane_exchange(tiles, lane8, lane_roll)):
+                send_buf[g // groups, f, pl.ds(row + 8 * part, 8), :] = tile
 
     def own_copy(ch, half):
         mine = place[half] * 2 + core
@@ -266,14 +252,14 @@
             send_buf.at[ch, 8 * half + mine], recv_buf.at[ch, half, mine], own_sem.at[ch, half]
         )
 
-    def first_hop(ch, half, step, flip, back=False):
+    def first_hop(ch, half, step, flip, back=False, rows=pl.ds(0, ROWS)):
         mine = place[half] * 2 + core
         group = lax.rem(place[half] + step, 4)
         core_at = lax.rem(core + flip, 2)
         peer = group * 2 + core_at
         return pltpu.make_async_remote_copy(
-            src_ref=send_buf.at[ch, 8 * half + peer],
-            dst_ref=recv_buf.at[ch, half, peer if back else mine],
+            src_ref=send_buf.at[ch, 8 * half + peer, rows],
+            dst_ref=recv_buf.at[ch, half, peer if back else mine, rows],
             send_sem=a_send.at[ch, half, 2 * step + flip],
             recv_sem=a_recv.at[ch, half, peer if back else mine],
             device_id=(ring, member(half, group, core_at)),
@@ -293,12 +279,15 @@
 
     first_order = ((1, 0), (3, 0), (1, 1), (3, 1), (2, 0), (2, 1), (0, 1))
 
-    def send_all(ch):
-        for half in range(2):
-            own_copy(ch, half).start()
+    parts = (pl.ds(0, 96), pl.ds(96, 64))
+
+    def send_part(ch, part):
+        if part == 1:
+            for half in range(2):
+                own_copy(ch, half).start()
         for step, flip in first_order:
             for half in range(2):
-                first_hop(ch, half, step, flip).start()
+                first_hop(ch, half, step, flip, rows=parts[part]).start()
 
     def hop(ch, half, side, s):
         sign = 1 if side == 0 else -1
@@ -386,14 +375,44 @@
         out_ref[4, ch, half] = total
         relay(ch, half, 1)
 
-    spanwise(0)
-    pl.semaphore_wait(barrier, 15)
-    send_all(0)
-    spanwise(1)
-    send_all(1)
+    def body(q, _):
+        @pl.when(q < groups // 2)
+        def _():
+            for s in range(2):
+                load(s, q).wait()
+
+        for odd in range(2):
+            regroup(2 * q + odd - 2, (z_even, z_odd)[odd])
+            if odd == 0:
+                products(hi_odd, lo_odd, z_odd)
+                residues(2 * q, hi_even, lo_even)
+            else:
+                products(hi_even, lo_even, z_even)
+                residues(2 * q + 1, hi_odd, lo_odd)
+
+        @pl.when(q == 3)
+        def _():
+            pl.semaphore_wait(barrier, 15)
+            send_part(0, 0)
+
+        @pl.when(q == 5)
+        def _():
+            send_part(0, 1)
+
+        @pl.when(q == 8)
+        def _():
+            send_part(1, 0)
+
+        return 0
+
+    lax.fori_loop(0, groups, body, 0)
+    regroup(2 * groups - 2, z_even)
+    products(hi_odd, lo_odd, z_odd)
+    regroup(2 * groups - 1, z_odd)
     tables_in.wait()
     axial(0, 0)
     axial(0, 1)
+    send_part(1, 1)
     gather(0, 0)
     gather(0, 1)
     axial(1, 0)
@@ -464,9 +483,12 @@
         scratch_shapes=[
             pltpu.VMEM((2, ROWS, NZ), f32),
             pltpu.VMEM((2 * KX, DEPTH), bf16),
-            pltpu.VMEM((CLASSES, ROWS, 512), bf16),
-            pltpu.VMEM((CLASSES, ROWS, 512), bf16),
-            pltpu.VMEM((CLASSES, ROWS, 128), f32),
+            pltpu.VMEM((CLASSES, 16, 512), bf16),
+            pltpu.VMEM((CLASSES, 16, 512), bf16),
+            pltpu.VMEM((CLASSES, 16, 512), bf16),
+            pltpu.VMEM((CLASSES, 16, 512), bf16),
+            pltpu.VMEM((CLASSES, 16, 128), f32),
+            pltpu.VMEM((CLASSES, 16, 128), f32),
             pltpu.VMEM((2, CLASSES, ROWS, 128), f32),
             pltpu.VMEM((2, 2, 8, ROWS, 128), f32),
             pltpu.VMEM((DEPTH, 256), bf16),

time: 72.5 us -> 71.5 us (0.986)
  Pallas kernels: 69.7 us -> 68.8 us
    pallas_call x1, Pallas kernels: 65.7 us -> 64.7 us  [local(): pl.pallas_call(transform_kernel, out_shape=jax.ShapeDtypeStruct((9,) + sl...]
where the time goes in v2:
time: 71.5 us; the launch traced here: 71.3 us
  Pallas kernels  68.8 us (96%)
  other arithmetic  1.49 us (2%)
    pallas_call x1, Pallas kernels, local(): pl.pallas_call(transform_kernel, out_shape=jax.ShapeDtypeStruct((9,) + sl...  64.7 us
    pallas_call x1, Pallas kernels, local(): pl.pallas_call(cross_kernel, grid=(2,), out_shape=(out, out), in_specs=[p...  4.04 us

profile of v2, /device:TPU:2, one launch (start us, length us, event | category | flops | bytes accessed | tf_op | source)
XLA Modules:
  0.0 71.3 jit_solution(17771577533778762725)
XLA Ops:
  0.6 0.8 %fusion = s32[80]{0:T(128)S(1)} fusion(s32[80,2]{0,1:T(2,128)} %param.8), kind=kLoop, calls=%fused_computation.4 | loop fusion | flops 240 | bytes 960 | tf_op jit(solution)/shard_map/sub | solution.py:515
  1.4 0.1 iota.36
  1.5 0.1 iota.37
  1.6 0.1 iota.32
  1.6 0.1 iota.33
  1.7 0.1 iota.35
  1.8 0.2 compare_reduce_fusion
  2.0 0.5 convert_element_type.3.flag_ref
  2.5 64.7 %transform.1.spec_ref = f32[9,2,2,2,16,512]{5,4,3,2,1,0:T(8,128)} custom-call(s32[16]{0:T(128)} %slot_ref.1, f32[2,160,3840]{2,1,0:T(8,128)} %vel_hbm.1, bf16[2,512,128]{2,1,0:T(8,128)(2,1)} %constant.21.clone.span_ref, f32[16,2,256]{2,1,0:T(2,128)} %constant.22.clone.twist_ref, bf16[1024,1024]{1,0:T(8,128)(2,1)} %constant.23.clone.axial_hbm), custom_call_target="tpu_custom_call" | custom-call | tf_op jit(solution)/shard_map/transform/pallas_call | solution.py:478
  67.3 4.0 %cross.1 = (f32[2,8,2,32,512]{4,3,2,1,0:T(8,128)}, f32[2,8,2,32,512]{4,3,2,1,0:T(8,128)}) custom-call(s32[2,16]{1,0:T(2,128)} %convert_element_type.3.flag_ref, f32[9,2,2,2,16,512]{5,4,3,2,1,0:T(8,128)} %transform.1.spec_ref), custom_call_target="tpu_custom_call" | custom-call | tf_op jit(solution)/shard_map/cross/pallas_call | solution.py:526
  (4 shorter events, 0.0 us)

commit v3 on v2

--- a/solution.py
+++ b/solution.py
@@ -61,7 +61,9 @@
         rows = slice(core * ROWS, core * ROWS + ROWS)
         parts += [ax_hi[:, rows], ax_hi[:, rows], ax_lo[:, rows]]
     parts.append(np.zeros((2 * KX, DEPTH - 6 * ROWS), bf16))
-    return np.stack(split_np(span)), twist, np.concatenate(parts, axis=1)
+    axial = np.concatenate(parts, axis=1).reshape(2, 2, KX // 2, DEPTH)
+    axial = np.ascontiguousarray(axial.transpose(1, 0, 2, 3)).reshape(2, KX, DEPTH)
+    return np.stack(split_np(span)), twist, axial
 
 
 def times(a, w):
@@ -112,22 +114,15 @@
     return out
 
 
-def twisted_classes(xs, cos_of, sin_of):
-    modes = real_fft(xs)
-    out = []
-    for c in range(CLASSES):
-        a, b = modes[c] if c <= 8 else modes[16 - c]
-        if c == 0:
-            out.append((a, jnp.zeros_like(a)))
-            continue
-        tc, ts = cos_of(c), sin_of(c)
-        if b is None:
-            out.append((a * tc, -(a * ts)))
-        elif c < 8:
-            out.append((a * tc + b * ts, b * tc - a * ts))
-        else:
-            out.append((a * tc - b * ts, -(b * tc + a * ts)))
-    return out
+def twisted_pair(modes, i, cos_of, sin_of):
+    stack = lambda u, v: jnp.concatenate([u, v], axis=0)
+    a, b = modes[i]
+    if i == 0:
+        e = modes[8][0]
+        return stack(a, e * cos_of(8)), stack(jnp.zeros_like(a), -(e * sin_of(8)))
+    tc, ts = cos_of(i), sin_of(i)
+    uc, us = cos_of(16 - i), sin_of(16 - i)
+    return stack(a * tc + b * ts, a * uc - b * us), stack(b * tc - a * ts, -(b * uc + a * us))
 
 
 def split(x):
@@ -192,9 +187,11 @@
                 pl.semaphore_signal(barrier, inc=1, device_id=(ring, peer), device_id_type=MESH)
     for other in (below, above):
         pl.semaphore_signal(barrier, inc=1, device_id=(other, me), device_id_type=MESH)
-    v_cat[pl.ds(6 * ROWS, DEPTH - 6 * ROWS), :] = jnp.zeros((DEPTH - 6 * ROWS, 256), bf16)
-
-    lane16 = lax.broadcasted_iota(jnp.int32, (16, 128), 1)
+    for half in range(2):
+        for s in range(2):
+            rest = pl.ds(6 * ROWS, DEPTH - 6 * ROWS)
+            v_cat[half, s, rest, :] = jnp.zeros((DEPTH - 6 * ROWS, 256), bf16)
+
     lane8 = lax.broadcasted_iota(jnp.int32, (8, 128), 1)
     groups = ROWS // 16
 
@@ -202,33 +199,32 @@
         slot = lax.rem(slot_ref[2 * ring + g // groups], 2)
         row = pl.multiple_of(lax.rem(g, groups) * 16, 16)
 
-        def tile(k):
-            at = (pl.ds(row, 16), pl.ds(128 * (k % 30), 128))
+        def tile(k, half):
+            at = (pl.ds(row + 8 * half, 8), pl.ds(128 * (k % 30), 128))
             return jnp.where(slot == 0, vel[(0,) + at], vel[(1,) + at])
 
-        for part in range(2):
+        for part, half in ((0, 0), (0, 1), (1, 0), (1, 1)):
             xs = []
             for j in range(CLASSES):
                 first, shift = divmod(SPAN * j + 128 * part, 128)
                 if shift == 0:
-                    xs.append(tile(first))
+                    xs.append(tile(first, half))
                     continue
                 xs.append(
                     jnp.where(
-                        lane16 < 128 - shift,
-                        lane_roll(tile(first), 128 - shift),
-                        lane_roll(tile(first + 1), 128 - shift),
+                        lane8 < 128 - shift,
+                        lane_roll(tile(first, half), 128 - shift),
+                        lane_roll(tile(first + 1, half), 128 - shift),
                     )
                 )
             cols = pl.ds(128 * part, 128)
-            cos_of = lambda c: jnp.broadcast_to(twist_ref[c, 0:1, cols], (16, 128))
-            sin_of = lambda c: jnp.broadcast_to(twist_ref[c, 1:2, cols], (16, 128))
-            for c, pair in enumerate(twisted_classes(xs, cos_of, sin_of)):
-                for which in range(2):
-                    high, low = split(pair[which])
+            cos_of = lambda c: jnp.broadcast_to(twist_ref[c, 0:1, cols], (8, 128))
+            sin_of = lambda c: jnp.broadcast_to(twist_ref[c, 1:2, cols], (8, 128))
+            modes = real_fft(xs)
+            for i in range(8):
+                for which, value in enumerate(twisted_pair(modes, i, cos_of, sin_of)):
                     at = pl.ds(256 * which + 128 * part, 128)
-                    y_hi[c, :, at] = high
-                    y_lo[c, :, at] = low
+                    y_hi[half, i, :, at], y_lo[half, i, :, at] = split(value)
 
     def products(y_hi, y_lo, z_buf):
         high = y_hi[...].reshape(CLASSES * 16, 512)
@@ -236,13 +232,13 @@
         total = jnp.dot(high, span_ref[0], preferred_element_type=f32)
         total += jnp.dot(low, span_ref[0], preferred_element_type=f32)
         total += jnp.dot(high, span_ref[1], preferred_element_type=f32)
-        z_buf[...] = total.reshape(CLASSES, 16, 128)
+        z_buf[...] = total.reshape(2, 8, 16, 128)
 
     def regroup(g, z_buf):
         g = jnp.maximum(g, 0)
         row = pl.multiple_of(lax.rem(g, groups) * 16, 16)
         for part in range(2):
-            tiles = [z_buf[c, pl.ds(8 * part, 8), :] for c in range(CLASSES)]
+            tiles = [z_buf[part, min(c, 16 - c) % 8, pl.ds(c // 8 * 8, 8), :] for c in range(CLASSES)]
             for f, tile in enumerate(lane_exchange(tiles, lane8, lane_roll)):
                 send_buf[g // groups, f, pl.ds(row + 8 * part, 8), :] = tile
 
@@ -266,36 +262,36 @@
             device_id_type=MESH,
         )
 
-    def second_hop(ch, half, step, back=False):
+    def second_hop(ch, half, kh, step, back=False):
         there = lax.rem(across[half] + step, 4)
         return pltpu.make_async_remote_copy(
-            src_ref=part_buf.at[ch, half, there],
-            dst_ref=sum_buf.at[ch, half, there if back else across[half]],
-            send_sem=b_send.at[ch, half, step],
-            recv_sem=b_recv.at[ch, half, there if back else across[half]],
+            src_ref=part_buf.at[ch, half, kh, there],
+            dst_ref=sum_buf.at[ch, half, kh, there if back else across[half]],
+            send_sem=b_send.at[ch, half, kh, step],
+            recv_sem=b_recv.at[ch, half, kh, there if back else across[half]],
             device_id=(ring, member(1 - half, there, core)),
             device_id_type=MESH,
         )
 
     first_order = ((1, 0), (3, 0), (1, 1), (3, 1), (2, 0), (2, 1), (0, 1))
 
-    parts = (pl.ds(0, 96), pl.ds(96, 64))
+    parts = (pl.ds(0, 64), pl.ds(64, 64), pl.ds(128, 32))
 
     def send_part(ch, part):
-        if part == 1:
+        if part == 2:
             for half in range(2):
                 own_copy(ch, half).start()
         for step, flip in first_order:
             for half in range(2):
                 first_hop(ch, half, step, flip, rows=parts[part]).start()
 
-    def hop(ch, half, side, s):
+    def hop(ch, half, kh, side, s):
         sign = 1 if side == 0 else -1
         return pltpu.make_async_remote_copy(
-            src_ref=out_ref.at[4 + sign * (s - 1), ch, half],
-            dst_ref=out_ref.at[4 + sign * s, ch, half],
-            send_sem=z_send.at[ch, half, side, s],
-            recv_sem=z_recv.at[ch, half, side, s],
+            src_ref=out_ref.at[4 + sign * (s - 1), ch, half, kh],
+            dst_ref=out_ref.at[4 + sign * s, ch, half, kh],
+            send_sem=z_send.at[ch, half, kh, side, s],
+            recv_sem=z_recv.at[ch, half, kh, side, s],
             device_id=(below if side == 0 else above, me),
             device_id_type=MESH,
         )
@@ -303,30 +299,34 @@
     def hops_of(ch, side):
         return 4 if ch == side else 3
 
-    def relay(ch, half, s):
+    def relay(ch, half, kh, s):
         for side in range(2):
             if 2 <= s <= hops_of(ch, side) + 1:
-                hop(ch, half, side, s - 1).wait_recv()
+                hop(ch, half, kh, side, s - 1).wait_recv()
             if s <= hops_of(ch, side):
-                hop(ch, half, side, s).start()
-
-    def axial(ch, half):
+                hop(ch, half, kh, side, s).start()
+
+    def relays(ch, s):
+        for kh in range(2):
+            for half in range(2):
+                relay(ch, half, kh, s)
+
+    def collect(ch, half):
         own_copy(ch, half).wait()
         for step, flip in first_order:
             first_hop(ch, half, step, flip, back=True).wait_recv()
-
-        def pair_step(s, _):
+        for s in range(2):
             for o in range(2):
                 cols = pl.ds(128 * o, 128)
                 for c in range(2):
                     high, low = split(recv_buf[ch, half, 4 * s + 2 * o + c])
-                    v_cat[pl.ds(3 * c * ROWS, ROWS), cols] = high
-                    v_cat[pl.ds((3 * c + 1) * ROWS, ROWS), cols] = low
-                    v_cat[pl.ds((3 * c + 2) * ROWS, ROWS), cols] = high
-            q_buf[s] = jnp.dot(axial_ref[...], v_cat[...], preferred_element_type=f32)
-            return 0
-
-        lax.fori_loop(0, 2, pair_step, 0)
+                    v_cat[half, s, pl.ds(3 * c * ROWS, ROWS), cols] = high
+                    v_cat[half, s, pl.ds((3 * c + 1) * ROWS, ROWS), cols] = low
+                    v_cat[half, s, pl.ds((3 * c + 2) * ROWS, ROWS), cols] = high
+
+    def axial(ch, half, kh):
+        for s in range(2):
+            q_buf[s] = jnp.dot(axial_ref[kh], v_cat[half, s], preferred_element_type=f32)
 
         k = lax.broadcasted_iota(jnp.int32, (16, 256), 0)
         o = lax.broadcasted_iota(jnp.int32, (16, 256), 1) // 128
@@ -342,11 +342,11 @@
         even = lane % 2 == 0
         mine = 8 * half + place[half] * 2 + core
         shift = lax.rem(128 - 8 * mine, 128)
-        for blk in range(KX // 16):
+        for blk in range(KX // 32):
             p = q = 0.0
             for s in range(2):
                 a = q_buf[s, pl.ds(16 * blk, 16), :]
-                b = q_buf[s, pl.ds(KX + 16 * blk, 16), :]
+                b = q_buf[s, pl.ds(KX // 2 + 16 * blk, 16), :]
                 p = p + (a * cos_of[s] - b * sin_of[s])
                 q = q + (a * sin_of[s] + b * cos_of[s])
             p = p[:, :128] + p[:, 128:]
@@ -354,7 +354,7 @@
             q = jnp.where(even, -q, q)
             turn_buf[0, pl.ds(16 * blk, 16), :] = lane_roll(p, shift)
             turn_buf[1, pl.ds(16 * blk, 16), :] = lane_roll(q, shift)
-        for blk in range(KX // 128):
+        for blk in range(2):
             rows = pl.ds(128 * blk, 128)
             for which in range(2):
                 flip_buf[which, blk] = turn_buf[which, rows, :].T
@@ -362,18 +362,18 @@
                 for ri in range(2):
                     straight = flip_buf[0, blk, pl.ds(2 * there + ri, 16, stride=8), :]
                     crossed = flip_buf[1, blk, pl.ds(2 * there + 1 - ri, 16, stride=8), :]
-                    part_buf[ch, half, there, ri, :, rows] = straight + crossed
+                    part_buf[ch, half, kh, there, ri, :, rows] = straight + crossed
         for step in (1, 3, 2):
-            second_hop(ch, half, step).start()
-
-    def gather(ch, half):
-        total = part_buf[ch, half, across[half]]
+            second_hop(ch, half, kh, step).start()
+
+    def gather(ch, half, kh):
+        total = part_buf[ch, half, kh, across[half]]
         for step in (1, 3, 2):
-            second_hop(ch, half, step, back=True).wait_recv()
+            second_hop(ch, half, kh, step, back=True).wait_recv()
         for step in range(1, 4):
-            total = total + sum_buf[ch, half, lax.rem(across[half] + step, 4)]
-        out_ref[4, ch, half] = total
-        relay(ch, half, 1)
+            total = total + sum_buf[ch, half, kh, lax.rem(across[half] + step, 4)]
+        out_ref[4, ch, half, kh] = total
+        relay(ch, half, kh, 1)
 
     def body(q, _):
         @pl.when(q < groups // 2)
@@ -390,18 +390,16 @@
                 products(hi_even, lo_even, z_even)
                 residues(2 * q + 1, hi_odd, lo_odd)
 
-        @pl.when(q == 3)
+        @pl.when(q == 2)
         def _():
             pl.semaphore_wait(barrier, 15)
             send_part(0, 0)
 
-        @pl.when(q == 5)
-        def _():
-            send_part(0, 1)
-
-        @pl.when(q == 8)
-        def _():
-            send_part(1, 0)
+        for at, ch, part in ((4, 0, 1), (5, 0, 2), (7, 1, 0)):
+
+            @pl.when(q == at)
+            def _():
+                send_part(ch, part)
 
         return 0
 
@@ -410,36 +408,43 @@
     products(hi_odd, lo_odd, z_odd)
     regroup(2 * groups - 1, z_odd)
     tables_in.wait()
-    axial(0, 0)
-    axial(0, 1)
+    collect(0, 0)
+    axial(0, 0, 0)
+    collect(0, 1)
+    axial(0, 1, 0)
     send_part(1, 1)
-    gather(0, 0)
-    gather(0, 1)
-    axial(1, 0)
-    relay(0, 0, 2)
-    relay(0, 1, 2)
-    axial(1, 1)
-    relay(0, 0, 3)
-    relay(0, 1, 3)
-    gather(1, 0)
-    gather(1, 1)
-    relay(0, 0, 4)
-    relay(0, 1, 4)
-    for s in range(2, 6):
-        if s == 3:
-            relay(0, 0, 5)
-            relay(0, 1, 5)
-        relay(1, 0, s)
-        relay(1, 1, s)
+    axial(0, 0, 1)
+    axial(0, 1, 1)
+    send_part(1, 2)
+    for kh in range(2):
+        for half in range(2):
+            gather(0, half, kh)
+    relays(0, 2)
+    collect(1, 0)
+    axial(1, 0, 0)
+    collect(1, 1)
+    axial(1, 1, 0)
+    relays(0, 3)
+    axial(1, 0, 1)
+    axial(1, 1, 1)
+    for kh in range(2):
+        for half in range(2):
+            gather(1, half, kh)
+    relays(0, 4)
+    relays(1, 2)
+    relays(0, 5)
+    for s in range(3, 6):
+        relays(1, s)
     for ch in range(2):
         for half in range(2):
             for step, flip in first_order:
                 first_hop(ch, half, step, flip).wait_send()
-            for step in (1, 3, 2):
-                second_hop(ch, half, step).wait_send()
-            for side in range(2):
-                for s in range(1, hops_of(ch, side) + 1):
-                    hop(ch, half, side, s).wait_send()
+            for kh in range(2):
+                for step in (1, 3, 2):
+                    second_hop(ch, half, kh, step).wait_send()
+                for side in range(2):
+                    for s in range(1, hops_of(ch, side) + 1):
+                        hop(ch, half, kh, side, s).wait_send()
 
 
 def cross_kernel(flag_ref, spec_ref, band_ref, partner_ref):
@@ -453,17 +458,19 @@
                 half = g // 2
                 row = pl.multiple_of(lax.rem(g, 2) * 8, 8)
                 at = pl.multiple_of(g * 8, 8)
-                re0 = spec_ref[4, i, half, 0, pl.ds(row, 8), :]
-                im0 = spec_ref[4, i, half, 1, pl.ds(row, 8), :]
-                for out, sign in ((band_ref, 1), (partner_ref, -1)):
-                    for d in range(BAND):
-                        off, odd = divmod(i + sign * d, 2)
-                        re1 = spec_ref[4 + off, odd, half, 0, pl.ds(row, 8), :]
-                        im1 = spec_ref[4 + off, odd, half, 1, pl.ds(row, 8), :]
-                        which = 0 if sign == 1 else 1
-                        ask = flag_ref[which, i * BAND + d] != 0
-                        out[0, d, 0, pl.ds(at, 8), :] = jnp.where(ask, re0 * re1 + im0 * im1, 0.0)
-                        out[0, d, 1, pl.ds(at, 8), :] = jnp.where(ask, im0 * re1 - re0 * im1, 0.0)
+                for kh in range(2):
+                    cols = pl.ds(KX // 2 * kh, KX // 2)
+                    re0 = spec_ref[4, i, half, kh, 0, pl.ds(row, 8), :]
+                    im0 = spec_ref[4, i, half, kh, 1, pl.ds(row, 8), :]
+                    for which, out, sign in ((0, band_ref, 1), (1, partner_ref, -1)):
+                        for d in range(BAND):
+                            off, odd = divmod(i + sign * d, 2)
+                            re1 = spec_ref[4 + off, odd, half, kh, 0, pl.ds(row, 8), :]
+                            im1 = spec_ref[4 + off, odd, half, kh, 1, pl.ds(row, 8), :]
+                            ask = flag_ref[which, i * BAND + d] != 0
+                            re, im = re0 * re1 + im0 * im1, im0 * re1 - re0 * im1
+                            out[0, d, 0, pl.ds(at, 8), cols] = jnp.where(ask, re, 0.0)
+                            out[0, d, 1, pl.ds(at, 8), cols] = jnp.where(ask, im, 0.0)
                 return 0
 
             lax.fori_loop(0, 4, pair, 0)
@@ -472,44 +479,46 @@
 def local(velocity, plane_slot, pair_list):
     span, twist, axial_cat = [jnp.asarray(t) for t in tables()]
     vmem = pl.BlockSpec(memory_space=pltpu.VMEM)
-    anywhere = pl.BlockSpec(memory_space=pl.ANY)
-    slab = (2, 2, 2, 16, KX)
+    hbm = pl.BlockSpec(memory_space=pltpu.HBM)
+    slab = (2, 2, 2, 2, 16, KX // 2)
     dma = pltpu.SemaphoreType.DMA
     spectra = pl.pallas_call(
         transform_kernel,
         out_shape=jax.ShapeDtypeStruct((9,) + slab, f32),
-        in_specs=[pl.BlockSpec(memory_space=pltpu.SMEM), anywhere, vmem, vmem, anywhere],
+        in_specs=[pl.BlockSpec(memory_space=pltpu.SMEM), hbm, vmem, vmem, hbm],
         out_specs=vmem,
         scratch_shapes=[
             pltpu.VMEM((2, ROWS, NZ), f32),
-            pltpu.VMEM((2 * KX, DEPTH), bf16),
-            pltpu.VMEM((CLASSES, 16, 512), bf16),
-            pltpu.VMEM((CLASSES, 16, 512), bf16),
-            pltpu.VMEM((CLASSES, 16, 512), bf16),
-            pltpu.VMEM((CLASSES, 16, 512), bf16),
-            pltpu.VMEM((CLASSES, 16, 128), f32),
-            pltpu.VMEM((CLASSES, 16, 128), f32),
+            pltpu.VMEM((2, KX, DEPTH), bf16),
+            pltpu.VMEM((2, 8, 16, 512), bf16),
+            pltpu.VMEM((2, 8, 16, 512), bf16),
+            pltpu.VMEM((2, 8, 16, 512), bf16),
+            pltpu.VMEM((2, 8, 16, 512), bf16),
+            pltpu.VMEM((2, 8, 16, 128), f32),
+            pltpu.VMEM((2, 8, 16, 128), f32),
             pltpu.VMEM((2, CLASSES, ROWS, 128), f32),
             pltpu.VMEM((2, 2, 8, ROWS, 128), f32),
-            pltpu.VMEM((DEPTH, 256), bf16),
-            pltpu.VMEM((2, 2 * KX, 256), f32),
-            pltpu.VMEM((2, KX, 128), f32),
-            pltpu.VMEM((2, KX // 128, 128, 128), f32),
-            pltpu.VMEM((2, 2, 4, 2, 16, KX), f32),
-            pltpu.VMEM((2, 2, 4, 2, 16, KX), f32),
+            pltpu.VMEM((2, 2, DEPTH, 256), bf16),
+            pltpu.VMEM((2, KX, 256), f32),
+            pltpu.VMEM((2, KX // 2, 128), f32),
+            pltpu.VMEM((2, 2, 128, 128), f32),
+            pltpu.VMEM((2, 2, 2, 4, 2, 16, KX // 2), f32),
+            pltpu.VMEM((2, 2, 2, 4, 2, 16, KX // 2), f32),
             dma((2, ROWS // 32)),
             dma,
             dma((2, 2)),
             dma((2, 2, 8)),
             dma((2, 2, 8)),
-            dma((2, 2, 4)),
-            dma((2, 2, 4)),
-            dma((2, 2, 2, 5)),
-            dma((2, 2, 2, 5)),
+            dma((2, 2, 2, 4)),
+            dma((2, 2, 2, 4)),
+            dma((2, 2, 2, 2, 5)),
+            dma((2, 2, 2, 2, 5)),
         ],
-        compiler_params=pltpu.CompilerParams(collective_id=0, has_side_effects=True),
+        compiler_params=pltpu.CompilerParams(
+            collective_id=0, has_side_effects=True, vmem_limit_bytes=40 * 1024 * 1024
+        ),
         name="transform",
-    )(plane_slot, velocity, span, twist, axial_cat)
+    )(plane_slot, pltpu.with_memory_space_constraint(velocity, pltpu.HBM), span, twist, pltpu.with_memory_space_constraint(axial_cat, pltpu.HBM))
 
     first_plane = lax.axis_index("plane") * 2
     code = pair_list[:, 0] * BAND + pair_list[:, 1] - pair_list[:, 0]
@@ -529,9 +538,10 @@
         out_shape=(out, out),
         in_specs=[
             pl.BlockSpec(memory_space=pltpu.SMEM),
-            pl.BlockSpec((9,) + slab, lambda i: (0,) * 6),
+            vmem,
         ],
         out_specs=(block, block),
+        compiler_params=pltpu.CompilerParams(vmem_limit_bytes=24 * 1024 * 1024),
         name="cross",
     )(flags, spectra)
     return (band_cross, partner_cross)

time: 71.5 us -> 69 us (0.965)
  Pallas kernels: 68.8 us -> 63.9 us
  local copies, waits for them, and re-layouts: 0.4 us -> 2.75 us
    pallas_call x1, Pallas kernels: 64.7 us -> 61 us  [local(): pl.pallas_call(transform_kernel, out_shape=jax.ShapeDtypeStruct((9,) + sl...]
    unnamed x0 -> x6, local copies, waits for them, and re-layouts: none -> 2.36 us
    pallas_call x1, Pallas kernels: 4.04 us -> 2.91 us  [local(): pl.pallas_call(cross_kernel, grid=(2,), out_shape=(out, out), in_specs=[p...]
where the time goes in v3:
time: 69 us; the launch traced here: 68.3 us
  Pallas kernels  63.9 us (93%)
  local copies, waits for them, and re-layouts  2.75 us (4%)
  other arithmetic  0.97 us (1%)
    pallas_call x1, Pallas kernels, local(): pl.pallas_call(transform_kernel, out_shape=jax.ShapeDtypeStruct((9,) + sl...  61 us
    pallas_call x1, Pallas kernels, local(): pl.pallas_call(cross_kernel, grid=(2,), out_shape=(out, out), in_specs=[p...  2.91 us
    unnamed x6, local copies, waits for them, and re-layouts  2.36 us

profile of v3, /device:TPU:2, one launch (start us, length us, event | category | flops | bytes accessed | tf_op | source)
XLA Modules:
  0.0 68.3 jit_solution(14448062961893279070)
XLA Ops:
  0.6 0.8 %fusion = s32[80]{0:T(128)S(1)} fusion(s32[80,2]{0,1:T(2,128)} %param.8), kind=kLoop, calls=%fused_computation.4 | loop fusion | flops 240 | bytes 960 | tf_op jit(solution)/shard_map/sub | solution.py:524
  1.4 0.1 iota.36
  1.5 0.1 iota.37
  1.6 0.1 iota.32
  1.6 0.1 iota.33
  1.7 0.1 iota.35
  1.8 0.2 compare_reduce_fusion
  2.0 0.0 copy-start
  2.0 0.9 %copy-done = bf16[2,512,128]{2,1,0:T(8,128)(2,1)S(1)} copy-done((bf16[2,512,128]{2,1,0:T(8,128)(2,1)S(1)}, bf16[2,512,128]{2,1,0:T(8,128)(2,1)}, u32[]{:S(2)}) %copy-start) | copy-done | bytes 262168
  3.0 0.0 copy-start.1
  3.0 0.8 %copy-done.1 = f32[16,2,256]{2,1,0:T(2,128)S(1)} copy-done((f32[16,2,256]{2,1,0:T(2,128)S(1)}, f32[16,2,256]{2,1,0:T(2,128)}, u32[]{:S(2)}) %copy-start.1) | copy-done | bytes 32792
  3.7 0.0 copy-start.2
  3.7 0.7 copy-done.2
  4.4 61.0 %transform.1.spec_ref = f32[9,2,2,2,2,16,256]{6,5,4,3,2,1,0:T(8,128)S(1)} custom-call(s32[16]{0:T(128)S(1)} %copy-done.2, f32[2,160,3840]{2,1,0:T(8,128)} %vel_hbm.1, bf16[2,512,128]{2,1,0:T(8,128)(2,1)S(1)} %copy-done, f32[16,2,256]{2,1,0:T(2,128)S(1)} %copy-done.1, bf16[2,512,1024]{2,1,0:T(8,128)(2,1)} %constant.23.clone.axial_hbm), custom_call_target="tpu_custom_call" | custom-call | tf_op jit(solution)/shard_map/transform/pallas_call | solution.py:485
  65.4 2.9 %cross.1 = (f32[2,8,2,32,512]{4,3,2,1,0:T(8,128)}, f32[2,8,2,32,512]{4,3,2,1,0:T(8,128)}) custom-call(s32[2,16]{1,0:T(2,128)S(1)} %convert_element_type.3.flag_ref, f32[9,2,2,2,2,16,256]{6,5,4,3,2,1,0:T(8,128)S(1)} %transform.1.spec_ref), custom_call_target="tpu_custom_call" | custom-call | tf_op jit(solution)/shard_map/cross/pallas_call | solution.py:535
  (5 shorter events, 0.0 us)
Async XLA Ops:
  2.0 1.0 %copy-start = (bf16[2,512,128]{2,1,0:T(8,128)(2,1)S(1)}, bf16[2,512,128]{2,1,0:T(8,128)(2,1)}, u32[]{:S(2)}) copy-start(bf16[2,512,128]{2,1,0:T(8,128)(2,1)} %constant.21.clone.span_ref) | copy-start | bytes 786436
  3.0 0.8 %copy-start.1 = (f32[16,2,256]{2,1,0:T(2,128)S(1)}, f32[16,2,256]{2,1,0:T(2,128)}, u32[]{:S(2)}) copy-start(f32[16,2,256]{2,1,0:T(2,128)} %constant.22.clone.twist_ref) | copy-start | bytes 98308
  3.7 0.7 copy-start.2

commit v4 on v3

--- a/solution.py
+++ b/solution.py
@@ -145,8 +145,8 @@
 
 
 def transform_kernel(
-    slot_ref, vel_hbm, span_ref, twist_ref, axial_hbm, out_ref,
-    vel, axial_ref, hi_even, lo_even, hi_odd, lo_odd, z_even, z_odd, send_buf, recv_buf, v_cat, q_buf, turn_buf,
+    slot_ref, vel_hbm, span_hbm, twist_hbm, axial_hbm, pair_ref, out_ref, flag_ref,
+    vel, span_ref, twist_ref, axial_ref, hi_even, lo_even, hi_odd, lo_odd, z_even, z_odd, send_buf, recv_buf, v_cat, q_buf, turn_buf,
     flip_buf, part_buf, sum_buf, load_sem, table_sem, own_sem, a_send, a_recv, b_send, b_recv,
     z_send, z_recv,
 ):
@@ -173,10 +173,15 @@
             vel_hbm.at[slot, rows], vel.at[slot, rows], load_sem.at[slot, part]
         )
 
+    twist_in = pltpu.make_async_copy(twist_hbm, twist_ref, table_sem.at[0])
+    span_in = pltpu.make_async_copy(span_hbm, span_ref, table_sem.at[1])
+    tables_in = pltpu.make_async_copy(axial_hbm, axial_ref, table_sem.at[2])
+    twist_in.start()
     for part in range(ROWS // 32):
         for slot in range(2):
             load(slot, part).start()
-    tables_in = pltpu.make_async_copy(axial_hbm, axial_ref, table_sem)
+        if part == 0:
+            span_in.start()
     tables_in.start()
     for half in range(2):
         for step in range(4):
@@ -301,15 +306,15 @@
 
     def relay(ch, half, kh, s):
         for side in range(2):
-            if 2 <= s <= hops_of(ch, side) + 1:
+            if s > hops_of(ch, side):
+                continue
+            if s > 1:
                 hop(ch, half, kh, side, s - 1).wait_recv()
-            if s <= hops_of(ch, side):
-                hop(ch, half, kh, side, s).start()
-
-    def relays(ch, s):
-        for kh in range(2):
-            for half in range(2):
-                relay(ch, half, kh, s)
+            hop(ch, half, kh, side, s).start()
+
+    def relays(ch, kh, s):
+        for half in range(2):
+            relay(ch, half, kh, s)
 
     def collect(ch, half):
         own_copy(ch, half).wait()
@@ -403,10 +408,20 @@
 
         return 0
 
+    twist_in.wait()
+    span_in.wait()
     lax.fori_loop(0, groups, body, 0)
     regroup(2 * groups - 2, z_even)
     products(hi_odd, lo_odd, z_odd)
     regroup(2 * groups - 1, z_odd)
+    index = lax.broadcasted_iota(jnp.int32, (1, 128), 1)
+    own_plane = 2 * ring + index // BAND % 2
+    gap = index % BAND
+    code = jnp.where(index < 2 * BAND, own_plane, own_plane - gap) * BAND + gap
+    lower = pair_ref[:, 0:1]
+    asked = lower * BAND + pair_ref[:, 1:2] - lower == code
+    asked = jnp.max(asked.astype(jnp.int32), axis=0, keepdims=True)
+    flag_ref[...] = jnp.where(own_plane - gap < 0, jnp.where(index < 2 * BAND, asked, 0), asked)
     tables_in.wait()
     collect(0, 0)
     axial(0, 0, 0)
@@ -414,27 +429,30 @@
     axial(0, 1, 0)
     send_part(1, 1)
     axial(0, 0, 1)
+    send_part(1, 2)
     axial(0, 1, 1)
-    send_part(1, 2)
     for kh in range(2):
         for half in range(2):
             gather(0, half, kh)
-    relays(0, 2)
+    for kh in range(2):
+        relays(0, kh, 2)
     collect(1, 0)
     axial(1, 0, 0)
+    relays(0, 0, 3)
     collect(1, 1)
     axial(1, 1, 0)
-    relays(0, 3)
+    relays(0, 1, 3)
     axial(1, 0, 1)
     axial(1, 1, 1)
-    for kh in range(2):
-        for half in range(2):
-            gather(1, half, kh)
-    relays(0, 4)
-    relays(1, 2)
-    relays(0, 5)
-    for s in range(3, 6):
-        relays(1, s)
+    relays(0, 0, 4)
+    for half in range(2):
+        gather(1, half, 0)
+    relays(0, 1, 4)
+    for half in range(2):
+        gather(1, half, 1)
+    for s in range(2, 5):
+        for kh in range(2):
+            relays(1, kh, s)
     for ch in range(2):
         for half in range(2):
             for step, flip in first_order:
@@ -443,21 +461,20 @@
                 for step in (1, 3, 2):
                     second_hop(ch, half, kh, step).wait_send()
                 for side in range(2):
+                    hop(ch, half, kh, side, hops_of(ch, side)).wait_recv()
                     for s in range(1, hops_of(ch, side) + 1):
                         hop(ch, half, kh, side, s).wait_send()
 
 
 def cross_kernel(flag_ref, spec_ref, band_ref, partner_ref):
-    ring = lax.axis_index("plane")
     own = pl.program_id(0)
+    half = pl.program_id(1)
     for i in range(2):
 
         @pl.when(own == i)
         def _():
             def pair(g, _):
-                half = g // 2
-                row = pl.multiple_of(lax.rem(g, 2) * 8, 8)
-                at = pl.multiple_of(g * 8, 8)
+                row = pl.multiple_of(g * 8, 8)
                 for kh in range(2):
                     cols = pl.ds(KX // 2 * kh, KX // 2)
                     re0 = spec_ref[4, i, half, kh, 0, pl.ds(row, 8), :]
@@ -467,13 +484,13 @@
                             off, odd = divmod(i + sign * d, 2)
                             re1 = spec_ref[4 + off, odd, half, kh, 0, pl.ds(row, 8), :]
                             im1 = spec_ref[4 + off, odd, half, kh, 1, pl.ds(row, 8), :]
-                            ask = flag_ref[which, i * BAND + d] != 0
+                            ask = flag_ref[0, (2 * which + i) * BAND + d] != 0
                             re, im = re0 * re1 + im0 * im1, im0 * re1 - re0 * im1
-                            out[0, d, 0, pl.ds(at, 8), cols] = jnp.where(ask, re, 0.0)
-                            out[0, d, 1, pl.ds(at, 8), cols] = jnp.where(ask, im, 0.0)
+                            out[0, d, 0, pl.ds(row, 8), cols] = jnp.where(ask, re, 0.0)
+                            out[0, d, 1, pl.ds(row, 8), cols] = jnp.where(ask, im, 0.0)
                 return 0
 
-            lax.fori_loop(0, 4, pair, 0)
+            lax.fori_loop(0, 2, pair, 0)
 
 
 def local(velocity, plane_slot, pair_list):
@@ -482,13 +499,18 @@
     hbm = pl.BlockSpec(memory_space=pltpu.HBM)
     slab = (2, 2, 2, 2, 16, KX // 2)
     dma = pltpu.SemaphoreType.DMA
-    spectra = pl.pallas_call(
+    spectra, flags = pl.pallas_call(
         transform_kernel,
-        out_shape=jax.ShapeDtypeStruct((9,) + slab, f32),
-        in_specs=[pl.BlockSpec(memory_space=pltpu.SMEM), hbm, vmem, vmem, hbm],
-        out_specs=vmem,
+        out_shape=(
+            jax.ShapeDtypeStruct((9,) + slab, f32),
+            jax.ShapeDtypeStruct((1, 128), jnp.int32),
+        ),
+        in_specs=[pl.BlockSpec(memory_space=pltpu.SMEM), hbm, hbm, hbm, hbm, vmem],
+        out_specs=(vmem, vmem),
         scratch_shapes=[
             pltpu.VMEM((2, ROWS, NZ), f32),
+            pltpu.VMEM((2, 512, 128), bf16),
+            pltpu.VMEM((CLASSES, 2, 256), f32),
             pltpu.VMEM((2, KX, DEPTH), bf16),
             pltpu.VMEM((2, 8, 16, 512), bf16),
             pltpu.VMEM((2, 8, 16, 512), bf16),
@@ -505,7 +527,7 @@
             pltpu.VMEM((2, 2, 2, 4, 2, 16, KX // 2), f32),
             pltpu.VMEM((2, 2, 2, 4, 2, 16, KX // 2), f32),
             dma((2, ROWS // 32)),
-            dma,
+            dma((3,)),
             dma((2, 2)),
             dma((2, 2, 8)),
             dma((2, 2, 8)),
@@ -518,23 +540,17 @@
             collective_id=0, has_side_effects=True, vmem_limit_bytes=40 * 1024 * 1024
         ),
         name="transform",
-    )(plane_slot, pltpu.with_memory_space_constraint(velocity, pltpu.HBM), span, twist, pltpu.with_memory_space_constraint(axial_cat, pltpu.HBM))
-
-    first_plane = lax.axis_index("plane") * 2
-    code = pair_list[:, 0] * BAND + pair_list[:, 1] - pair_list[:, 0]
-    own = first_plane + lax.broadcasted_iota(jnp.int32, (2, BAND), 0)
-    gap = lax.broadcasted_iota(jnp.int32, (2, BAND), 1)
-    up = own * BAND + gap
-    down = jnp.where(own >= gap, (own - gap) * BAND + gap, -1)
-    asked = jnp.stack([up, down]).reshape(2, 2 * BAND, 1)
-    flags = jnp.any(asked == code, axis=2).astype(jnp.int32)
+    )(*[
+        pltpu.with_memory_space_constraint(array, pltpu.HBM)
+        for array in (plane_slot, velocity, span, twist, axial_cat, pair_list)
+    ])
 
     share = KZ // PEERS
     out = jax.ShapeDtypeStruct((2, BAND, 2, share, KX), f32)
-    block = pl.BlockSpec((1, BAND, 2, share, KX), lambda i: (i, 0, 0, 0, 0))
+    block = pl.BlockSpec((1, BAND, 2, share // 2, KX), lambda i, h: (i, 0, 0, h, 0))
     band_cross, partner_cross = pl.pallas_call(
         cross_kernel,
-        grid=(2,),
+        grid=(2, 2),
         out_shape=(out, out),
         in_specs=[
             pl.BlockSpec(memory_space=pltpu.SMEM),

time: 69 us -> 67.6 us (0.980)
  Pallas kernels: 63.9 us -> 65.3 us
  local copies, waits for them, and re-layouts: 2.75 us -> 1.39 us
  other arithmetic: 0.97 us -> 0 us
    pallas_call x2, Pallas kernels: 63.9 us -> 65.3 us  [the longest x1 62.1 us: local(): pl.pallas_call(transform_kernel, out_shape=(jax.ShapeDtypeStruct((9,) + s...]
    unnamed x6 -> x1, local copies, waits for them, and re-layouts: 2.36 us -> 1.39 us
    sub x1 -> x0, other arithmetic: 0.76 us -> none  [local(): code = pair_list[:, 0] * BAND + pair_list[:, 1] - pair_list[:, 0]]
where the time goes in v4:
time: 67.6 us; the launch traced here: 67.3 us
  Pallas kernels  65.3 us (97%)
  local copies, waits for them, and re-layouts  1.39 us (2%)
    pallas_call x1, Pallas kernels, local(): pl.pallas_call(transform_kernel, out_shape=(jax.ShapeDtypeStruct((9,) + s...  62.1 us
    pallas_call x1, Pallas kernels, local(): pl.pallas_call(cross_kernel, grid=(2, 2), out_shape=(out, out), in_specs=...  3.18 us
    unnamed x1, local copies, waits for them, and re-layouts  1.39 us

profile of v4, /device:TPU:2, one launch (start us, length us, event | category | flops | bytes accessed | tf_op | source)
XLA Modules:
  0.0 67.3 jit_solution(14885797051639369954)
XLA Ops:
  0.6 1.4 %copy.8.pair_ref = s32[80,2]{1,0:T(8,128)} copy(s32[80,2]{0,1:T(2,128)} %param.8) | data formatting | bytes 1280 | tf_op args[2]
  2.0 62.1 %transform.1 = (f32[9,2,2,2,2,16,256]{6,5,4,3,2,1,0:T(8,128)S(1)}, s32[1,128]{1,0:T(1,128)S(1)}) custom-call(s32[16]{0:T(128)} %slot_ref.1, f32[2,160,3840]{2,1,0:T(8,128)} %vel_hbm.1, bf16[2,512,128]{2,1,0:T(8,128)(2,1)} %constant.6.clone.span_hbm, f32[16,2,256]{2,1,0:T(2,128)} %constant.7.clone.twist_hbm, bf16[2,512,1024]{2,1,0:T(8,128)(2,1)} %constant.8.clone.axial_hbm, ...), custom_call_target="tpu_custom_call" | custom-call | tf_op jit(solution)/shard_map/transform/pallas_call | solution.py:502
  64.1 3.2 %cross.1 = (f32[2,8,2,32,512]{4,3,2,1,0:T(8,128)}, f32[2,8,2,32,512]{4,3,2,1,0:T(8,128)}) custom-call(s32[1,128]{1,0:T(1,128)S(1)} %get-tuple-element.4.flag_ref, f32[9,2,2,2,2,16,256]{6,5,4,3,2,1,0:T(8,128)S(1)} %get-tuple-element.5.spec_ref), custom_call_target="tpu_custom_call" | custom-call | tf_op jit(solution)/shard_map/cross/pallas_call | solution.py:551

commit v5 on v4

--- a/solution.py
+++ b/solution.py
@@ -63,7 +63,7 @@
     parts.append(np.zeros((2 * KX, DEPTH - 6 * ROWS), bf16))
     axial = np.concatenate(parts, axis=1).reshape(2, 2, KX // 2, DEPTH)
     axial = np.ascontiguousarray(axial.transpose(1, 0, 2, 3)).reshape(2, KX, DEPTH)
-    return np.stack(split_np(span)), twist, axial
+    return np.concatenate(split_np(span), axis=1), twist, axial
 
 
 def times(a, w):
@@ -234,9 +234,9 @@
     def products(y_hi, y_lo, z_buf):
         high = y_hi[...].reshape(CLASSES * 16, 512)
         low = y_lo[...].reshape(CLASSES * 16, 512)
-        total = jnp.dot(high, span_ref[0], preferred_element_type=f32)
-        total += jnp.dot(low, span_ref[0], preferred_element_type=f32)
-        total += jnp.dot(high, span_ref[1], preferred_element_type=f32)
+        both = jnp.dot(high, span_ref[...], preferred_element_type=f32)
+        total = both[:, :128] + both[:, 128:]
+        total += jnp.dot(low, span_ref[:, pl.ds(0, 128)], preferred_element_type=f32)
         z_buf[...] = total.reshape(2, 8, 16, 128)
 
     def regroup(g, z_buf):
@@ -280,7 +280,7 @@
 
     first_order = ((1, 0), (3, 0), (1, 1), (3, 1), (2, 0), (2, 1), (0, 1))
 
-    parts = (pl.ds(0, 64), pl.ds(64, 64), pl.ds(128, 32))
+    parts = (pl.ds(0, 32), pl.ds(32, 64), pl.ds(96, 64))
 
     def send_part(ch, part):
         if part == 2:
@@ -395,12 +395,12 @@
                 products(hi_even, lo_even, z_even)
                 residues(2 * q + 1, hi_odd, lo_odd)
 
-        @pl.when(q == 2)
+        @pl.when(q == 1)
         def _():
             pl.semaphore_wait(barrier, 15)
             send_part(0, 0)
 
-        for at, ch, part in ((4, 0, 1), (5, 0, 2), (7, 1, 0)):
+        for at, ch, part in ((3, 0, 1), (5, 0, 2), (6, 1, 0), (8, 1, 1)):
 
             @pl.when(q == at)
             def _():
@@ -414,22 +414,22 @@
     regroup(2 * groups - 2, z_even)
     products(hi_odd, lo_odd, z_odd)
     regroup(2 * groups - 1, z_odd)
-    index = lax.broadcasted_iota(jnp.int32, (1, 128), 1)
+    index = lax.broadcasted_iota(jnp.int32, (4 * BAND, 1), 0)
     own_plane = 2 * ring + index // BAND % 2
     gap = index % BAND
     code = jnp.where(index < 2 * BAND, own_plane, own_plane - gap) * BAND + gap
-    lower = pair_ref[:, 0:1]
-    asked = lower * BAND + pair_ref[:, 1:2] - lower == code
-    asked = jnp.max(asked.astype(jnp.int32), axis=0, keepdims=True)
-    flag_ref[...] = jnp.where(own_plane - gap < 0, jnp.where(index < 2 * BAND, asked, 0), asked)
+    lower = pair_ref[0:1, :]
+    asked = lower * BAND + pair_ref[1:2, :] - lower == code
+    asked = jnp.max(jnp.where(asked, 1.0, 0.0), axis=1, keepdims=True)
+    asked = jnp.where((index >= 2 * BAND) & (own_plane < gap), 0.0, asked)
+    flag_ref[...] = jnp.broadcast_to(asked, (4 * BAND, KX // 2))
     tables_in.wait()
     collect(0, 0)
     axial(0, 0, 0)
     collect(0, 1)
     axial(0, 1, 0)
-    send_part(1, 1)
+    send_part(1, 2)
     axial(0, 0, 1)
-    send_part(1, 2)
     axial(0, 1, 1)
     for kh in range(2):
         for half in range(2):
@@ -484,7 +484,8 @@
                             off, odd = divmod(i + sign * d, 2)
                             re1 = spec_ref[4 + off, odd, half, kh, 0, pl.ds(row, 8), :]
                             im1 = spec_ref[4 + off, odd, half, kh, 1, pl.ds(row, 8), :]
-                            ask = flag_ref[0, (2 * which + i) * BAND + d] != 0
+                            at = (2 * which + i) * BAND + d
+                            ask = jnp.broadcast_to(flag_ref[at : at + 1, :], (8, KX // 2)) != 0.0
                             re, im = re0 * re1 + im0 * im1, im0 * re1 - re0 * im1
                             out[0, d, 0, pl.ds(row, 8), cols] = jnp.where(ask, re, 0.0)
                             out[0, d, 1, pl.ds(row, 8), cols] = jnp.where(ask, im, 0.0)
@@ -503,13 +504,13 @@
         transform_kernel,
         out_shape=(
             jax.ShapeDtypeStruct((9,) + slab, f32),
-            jax.ShapeDtypeStruct((1, 128), jnp.int32),
+            jax.ShapeDtypeStruct((4 * BAND, KX // 2), f32),
         ),
         in_specs=[pl.BlockSpec(memory_space=pltpu.SMEM), hbm, hbm, hbm, hbm, vmem],
         out_specs=(vmem, vmem),
         scratch_shapes=[
             pltpu.VMEM((2, ROWS, NZ), f32),
-            pltpu.VMEM((2, 512, 128), bf16),
+            pltpu.VMEM((512, 256), bf16),
             pltpu.VMEM((CLASSES, 2, 256), f32),
             pltpu.VMEM((2, KX, DEPTH), bf16),
             pltpu.VMEM((2, 8, 16, 512), bf16),
@@ -542,7 +543,7 @@
         name="transform",
     )(*[
         pltpu.with_memory_space_constraint(array, pltpu.HBM)
-        for array in (plane_slot, velocity, span, twist, axial_cat, pair_list)
+        for array in (plane_slot, velocity, span, twist, axial_cat, pair_list.T)
     ])
 
     share = KZ // PEERS
@@ -552,10 +553,7 @@
         cross_kernel,
         grid=(2, 2),
         out_shape=(out, out),
-        in_specs=[
-            pl.BlockSpec(memory_space=pltpu.SMEM),
-            vmem,
-        ],
+        in_specs=[vmem, vmem],
         out_specs=(block, block),
         compiler_params=pltpu.CompilerParams(vmem_limit_bytes=24 * 1024 * 1024),
         name="cross",

time: 67.6 us -> 63.9 us (0.945)
  Pallas kernels: 65.3 us -> 63.1 us
  local copies, waits for them, and re-layouts: 1.39 us -> 0 us
    pallas_call x1, Pallas kernels: 62.1 us -> 60.4 us  [local(): pl.pallas_call(transform_kernel, out_shape=(jax.ShapeDtypeStruct((9,) + s...]
    unnamed x1 -> x0, local copies, waits for them, and re-layouts: 1.39 us -> none
where the time goes in v5:
time: 63.9 us; the launch traced here: 63.7 us
  Pallas kernels  63.1 us (99%)
  between operations  0.64 us (1%)
    pallas_call x1, Pallas kernels, local(): pl.pallas_call(transform_kernel, out_shape=(jax.ShapeDtypeStruct((9,) + s...  60.4 us
    pallas_call x1, Pallas kernels, local(): pl.pallas_call(cross_kernel, grid=(2, 2), out_shape=(out, out), in_specs=...  2.63 us

profile of v5, /device:TPU:2, one launch (start us, length us, event | category | flops | bytes accessed | tf_op | source)
XLA Modules:
  0.0 63.7 jit_solution(11553041476010118959)
XLA Ops:
  0.6 60.4 %transform.1 = (f32[9,2,2,2,2,16,256]{6,5,4,3,2,1,0:T(8,128)S(1)}, f32[32,256]{1,0:T(8,128)S(1)}) custom-call(s32[16]{0:T(128)} %slot_ref.1, f32[2,160,3840]{2,1,0:T(8,128)} %vel_hbm.1, bf16[512,256]{1,0:T(8,128)(2,1)} %constant.6.clone.span_hbm, f32[16,2,256]{2,1,0:T(2,128)} %constant.7.clone.twist_hbm, bf16[2,512,1024]{2,1,0:T(8,128)(2,1)} %constant.8.clone.axial_hbm, ...), custom_call_target="tpu_custom_call" | custom-call | tf_op jit(solution)/shard_map/transform/pallas_call | solution.py:503
  61.1 2.6 %cross.1 = (f32[2,8,2,32,512]{4,3,2,1,0:T(8,128)}, f32[2,8,2,32,512]{4,3,2,1,0:T(8,128)}) custom-call(f32[32,256]{1,0:T(8,128)S(1)} %get-tuple-element.4.flag_ref, f32[9,2,2,2,2,16,256]{6,5,4,3,2,1,0:T(8,128)S(1)} %get-tuple-element.5.spec_ref), custom_call_target="tpu_custom_call" | custom-call | tf_op jit(solution)/shard_map/cross/pallas_call | solution.py:552

commit v6 on v5

--- a/solution.py
+++ b/solution.py
@@ -428,9 +428,9 @@
     axial(0, 0, 0)
     collect(0, 1)
     axial(0, 1, 0)
-    send_part(1, 2)
     axial(0, 0, 1)
     axial(0, 1, 1)
+    send_part(1, 2)
     for kh in range(2):
         for half in range(2):
             gather(0, half, kh)

time: 63.9 us -> 62.3 us (0.975)
  Pallas kernels: 63.1 us -> 61.6 us
    pallas_call x1, Pallas kernels: 60.4 us -> 59 us  [local(): pl.pallas_call(transform_kernel, out_shape=(jax.ShapeDtypeStruct((9,) + s...]
where the time goes in v6:
time: 62.3 us; the launch traced here: 62.2 us
  Pallas kernels  61.6 us (99%)
  between operations  0.64 us (1%)
    pallas_call x1, Pallas kernels, local(): pl.pallas_call(transform_kernel, out_shape=(jax.ShapeDtypeStruct((9,) + s...  59 us
    pallas_call x1, Pallas kernels, local(): pl.pallas_call(cross_kernel, grid=(2, 2), out_shape=(out, out), in_specs=...  2.63 us

profile of v6, /device:TPU:2, one launch (start us, length us, event | category | flops | bytes accessed | tf_op | source)
XLA Modules:
  0.0 62.2 jit_solution(4114320582081732183)
XLA Ops:
  0.6 59.0 %transform.1 = (f32[9,2,2,2,2,16,256]{6,5,4,3,2,1,0:T(8,128)S(1)}, f32[32,256]{1,0:T(8,128)S(1)}) custom-call(s32[16]{0:T(128)} %slot_ref.1, f32[2,160,3840]{2,1,0:T(8,128)} %vel_hbm.1, bf16[512,256]{1,0:T(8,128)(2,1)} %constant.6.clone.span_hbm, f32[16,2,256]{2,1,0:T(2,128)} %constant.7.clone.twist_hbm, bf16[2,512,1024]{2,1,0:T(8,128)(2,1)} %constant.8.clone.axial_hbm, ...), custom_call_target="tpu_custom_call" | custom-call | tf_op jit(solution)/shard_map/transform/pallas_call | solution.py:503
  59.6 2.6 %cross.1 = (f32[2,8,2,32,512]{4,3,2,1,0:T(8,128)}, f32[2,8,2,32,512]{4,3,2,1,0:T(8,128)}) custom-call(f32[32,256]{1,0:T(8,128)S(1)} %get-tuple-element.4.flag_ref, f32[9,2,2,2,2,16,256]{6,5,4,3,2,1,0:T(8,128)S(1)} %get-tuple-element.5.spec_ref), custom_call_target="tpu_custom_call" | custom-call | tf_op jit(solution)/shard_map/cross/pallas_call | solution.py:552

commit v7 on v6

--- a/solution.py
+++ b/solution.py
@@ -450,20 +450,31 @@
     relays(0, 1, 4)
     for half in range(2):
         gather(1, half, 1)
-    for s in range(2, 5):
-        for kh in range(2):
-            relays(1, kh, s)
-    for ch in range(2):
+    def sent_by(ch):
         for half in range(2):
             for step, flip in first_order:
                 first_hop(ch, half, step, flip).wait_send()
             for kh in range(2):
                 for step in (1, 3, 2):
                     second_hop(ch, half, kh, step).wait_send()
+
+    def relayed(ch):
+        for half in range(2):
+            for kh in range(2):
                 for side in range(2):
                     hop(ch, half, kh, side, hops_of(ch, side)).wait_recv()
                     for s in range(1, hops_of(ch, side) + 1):
                         hop(ch, half, kh, side, s).wait_send()
+
+    sent_by(0)
+    for s in range(2, 5):
+        for kh in range(2):
+            relays(1, kh, s)
+        if s == 2:
+            sent_by(1)
+        if s == 3:
+            relayed(0)
+    relayed(1)
 
 
 def cross_kernel(flag_ref, spec_ref, band_ref, partner_ref):

time: 62.3 us -> 62.3 us (level)
  no operation moved by 1% of the time
where the time goes in v7:
time: 62.3 us; the launch traced here: 62.2 us
  Pallas kernels  61.6 us (99%)
  between operations  0.64 us (1%)
    pallas_call x1, Pallas kernels, local(): pl.pallas_call(transform_kernel, out_shape=(jax.ShapeDtypeStruct((9,) + s...  59 us
    pallas_call x1, Pallas kernels, local(): pl.pallas_call(cross_kernel, grid=(2, 2), out_shape=(out, out), in_specs=...  2.63 us

profile of v7, /device:TPU:2, one launch (start us, length us, event | category | flops | bytes accessed | tf_op | source)
XLA Modules:
  0.0 62.2 jit_solution(8906193887349822832)
XLA Ops:
  0.6 59.0 %transform.1 = (f32[9,2,2,2,2,16,256]{6,5,4,3,2,1,0:T(8,128)S(1)}, f32[32,256]{1,0:T(8,128)S(1)}) custom-call(s32[16]{0:T(128)} %slot_ref.1, f32[2,160,3840]{2,1,0:T(8,128)} %vel_hbm.1, bf16[512,256]{1,0:T(8,128)(2,1)} %constant.6.clone.span_hbm, f32[16,2,256]{2,1,0:T(2,128)} %constant.7.clone.twist_hbm, bf16[2,512,1024]{2,1,0:T(8,128)(2,1)} %constant.8.clone.axial_hbm, ...), custom_call_target="tpu_custom_call" | custom-call | tf_op jit(solution)/shard_map/transform/pallas_call | solution.py:514
  59.6 2.6 %cross.1 = (f32[2,8,2,32,512]{4,3,2,1,0:T(8,128)}, f32[2,8,2,32,512]{4,3,2,1,0:T(8,128)}) custom-call(f32[32,256]{1,0:T(8,128)S(1)} %get-tuple-element.4.flag_ref, f32[9,2,2,2,2,16,256]{6,5,4,3,2,1,0:T(8,128)S(1)} %get-tuple-element.5.spec_ref), custom_call_target="tpu_custom_call" | custom-call | tf_op jit(solution)/shard_map/cross/pallas_call | solution.py:563
